TPU v7x, 32 devices: a whole 2x2x4 slice. The times are simulated.
32 devices in a mesh: dp: 2 (over y), ctx: 4 (over z), mp: 4 (over x, core).
Axes of the slice: x: 2, y: 2, z: 4, core: 2. Of those that a mesh axis runs over, the one named last changes fastest.
Arguments:
- hidden_in: bfloat16 [2, 4, 2048, 2048], P(None, 'dp', 'ctx'), may hold values from -6 to 6
- teacher: bfloat16 [2, 4, 2048, 2048], P(None, 'dp', 'ctx'), may hold values from -6 to 6
- lengths: int32 [2, 4], replicated, may hold values from 512 to 2048, as said below
- query_weight: bfloat16 [2048, 2048], P(('dp', 'ctx'), 'mp'), may hold values from -0.125 to 0.125
- key_weight: bfloat16 [2048, 2048], P(('dp', 'ctx'), 'mp'), may hold values from -0.125 to 0.125
- value_weight: bfloat16 [2048, 2048], P(('dp', 'ctx'), 'mp'), may hold values from -0.125 to 0.125
- out_weight: bfloat16 [2048, 2048], P('mp', ('dp', 'ctx')), may hold values from -2 to 2
- gate_weight: bfloat16 [2048, 5504], P(('dp', 'ctx'), 'mp'), may hold values from -0.125 to 0.125
- up_weight: bfloat16 [2048, 5504], P(('dp', 'ctx'), 'mp'), may hold values from -0.125 to 0.125
- down_weight: bfloat16 [5504, 2048], P('mp', ('dp', 'ctx')), may hold values from -0.078125 to 0.078125
- attention_gain: bfloat16 [2048], P(('dp', 'ctx')), may hold values from 0.25 to 1.75
- feed_gain: bfloat16 [2048], P(('dp', 'ctx')), may hold values from 0.25 to 1.75
Outputs:
- out_hidden: bfloat16 [2, 4, 2048, 2048], P(None, 'dp', 'ctx')
- loss: float32 [], replicated
- grad_hidden: bfloat16 [2, 4, 2048, 2048], P(None, 'dp', 'ctx')
- grad_query_weight: float32 [2048, 2048], P(('dp', 'ctx'), 'mp')
- grad_key_weight: float32 [2048, 2048], P(('dp', 'ctx'), 'mp')
- grad_value_weight: float32 [2048, 2048], P(('dp', 'ctx'), 'mp')
- grad_out_weight: float32 [2048, 2048], P('mp', ('dp', 'ctx'))
- grad_gate_weight: float32 [2048, 5504], P(('dp', 'ctx'), 'mp')
- grad_up_weight: float32 [2048, 5504], P(('dp', 'ctx'), 'mp')
- grad_down_weight: float32 [5504, 2048], P('mp', ('dp', 'ctx'))
- grad_attention_gain: float32 [2048], P(('dp', 'ctx'))
- grad_feed_gain: float32 [2048], P(('dp', 'ctx'))
Inputs may be any that keep to these rules, and one draw needn't show every extreme that they name: Each micro-batch has one slot with all 2048 positions valid; the valid positions of a slot are its first lengths[m, s] ones.
All inputs are finite; a program needn't handle non-finite values.
Results may differ from a plain program's by a relative error of at most 0.012.
Values may be sent and summed in bfloat16 or wider, within the bound.
No kernel may reach another device: no remote copies, remote signals or barrier semaphores. Data moves between devices by JAX's collectives and lax.ppermute only.
A program may use at most 384 MiB of HBM per device.

v0:
```python
import jax
import jax.numpy as jnp
from jax import lax
from jax.sharding import PartitionSpec as P

HEAD_DIM = 128
WINDOW = 1024
SEQ = 2048


EPS = 1e-06
NEGATIVE = -1e30


def shifted(value, axis, steps):
    count = lax.axis_size(axis)
    leading, last = (max(0, -steps), min(count, count - steps))
    return lax.ppermute(value, axis, [(source, source + steps) for source in range(leading, last)])


def norm_rows(v):
    return v * lax.rsqrt(jnp.mean(v * v, axis=-1, keepdims=True) + EPS)


def silu(v):
    return v * jax.nn.sigmoid(v)


def plain_dot(left, right):
    return jnp.dot(left, right, preferred_element_type=jnp.float32)


def left_dot(left, right):
    return lax.dot_general(
        left, right, (((0,), (0,)), ((), ())), preferred_element_type=jnp.float32
    )


def right_dot(left, right):
    return lax.dot_general(
        left, right, (((1,), (1,)), ((), ())), preferred_element_type=jnp.float32
    )


def gain_norm(values, gain):
    return norm_rows(values) * gain


def gated_unit(gate, upper):
    return silu(gate) * upper


def on_device(
    hidden_in,
    teacher,
    lengths,
    query_weight,
    key_weight,
    value_weight,
    out_weight,
    gate_weight,
    up_weight,
    down_weight,
    attention_gain,
    feed_gain,
):
    n_micro, n_slot, group, width = hidden_in.shape
    local_heads = query_weight.shape[1] // HEAD_DIM
    head_cols = query_weight.shape[1]
    reach = WINDOW // group
    extent = (reach + 1) * group
    rows = n_slot * group
    scale = HEAD_DIM ** (-0.5)
    ctx_index = lax.axis_index("ctx")
    dp_index = lax.axis_index("dp")
    count = jnp.sum(lengths).astype(jnp.float32)
    factor = lengths.shape[0] * lengths.shape[1] * SEQ / count
    own_lengths = lax.dynamic_slice_in_dim(lengths, dp_index * n_slot, n_slot, 1)
    positions = ctx_index * group + jnp.arange(group, dtype=jnp.int32)
    key_positions = ctx_index * group - reach * group + jnp.arange(extent, dtype=jnp.int32)
    distance = positions[:, None] - key_positions[None, :]
    in_window = (distance >= 0) & (distance < WINDOW) & (key_positions[None, :] >= 0)

    def fetch_attention():
        return (
            lax.all_gather(query_weight, ("dp", "ctx"), axis=0, tiled=True),
            lax.all_gather(key_weight, ("dp", "ctx"), axis=0, tiled=True),
            lax.all_gather(value_weight, ("dp", "ctx"), axis=0, tiled=True),
            lax.all_gather(out_weight, ("dp", "ctx"), axis=1, tiled=True),
            lax.all_gather(attention_gain, ("dp", "ctx"), axis=0, tiled=True),
        )

    def fetch_feed():
        return (
            lax.all_gather(gate_weight, ("dp", "ctx"), axis=0, tiled=True),
            lax.all_gather(up_weight, ("dp", "ctx"), axis=0, tiled=True),
            lax.all_gather(down_weight, ("dp", "ctx"), axis=1, tiled=True),
            lax.all_gather(feed_gain, ("dp", "ctx"), axis=0, tiled=True),
        )

    acc_query = jnp.zeros((width, head_cols), jnp.float32)
    acc_key = jnp.zeros((width, head_cols), jnp.float32)
    acc_value = jnp.zeros((width, head_cols), jnp.float32)
    acc_out = jnp.zeros((head_cols, width), jnp.float32)
    acc_gate = jnp.zeros((width, gate_weight.shape[1]), jnp.float32)
    acc_up = jnp.zeros((width, gate_weight.shape[1]), jnp.float32)
    acc_down = jnp.zeros((gate_weight.shape[1], width), jnp.float32)
    acc_gain_a = jnp.zeros((width,), jnp.float32)
    acc_gain_f = jnp.zeros((width,), jnp.float32)
    loss_part = jnp.zeros((), jnp.float32)
    results = []
    input_grads = []

    def scores_of(queries_four, keys_ext, allowed):
        raw = (
            jnp.einsum(
                "sqhd,skhd->shqk", queries_four, keys_ext, preferred_element_type=jnp.float32
            )
            * scale
        )
        return jnp.where(allowed[:, None], raw, NEGATIVE)

    for micro in range(n_micro):
        slot_len = own_lengths[micro]
        valid = positions[None, :] < slot_len[:, None]
        key_ok = (key_positions[None, None, :] < slot_len[:, None, None]) | (distance == 0)[None]
        allowed = in_window[None] & key_ok
        valid_rows = valid.reshape(rows, 1).astype(jnp.float32)
        attention_set = fetch_attention()
        full_query, full_key, full_value, full_out, full_gain_a = attention_set
        gain_a = full_gain_a.astype(jnp.float32)
        x_in = hidden_in[micro].reshape(rows, width).astype(jnp.float32)
        normed_a = gain_norm(x_in, gain_a).astype(jnp.bfloat16)
        queries = plain_dot(normed_a, full_query).astype(jnp.bfloat16)
        keys = plain_dot(normed_a, full_key).astype(jnp.bfloat16)
        values = plain_dot(normed_a, full_value).astype(jnp.bfloat16)
        keys_slot = keys.reshape(n_slot, group, head_cols)
        values_slot = values.reshape(n_slot, group, head_cols)
        key_parts = []
        value_parts = []
        for back in range(reach, 0, -1):
            got_keys, got_values = shifted((keys_slot, values_slot), "ctx", back)
            key_parts.append(got_keys)
            value_parts.append(got_values)
        keys_ext = jnp.concatenate(key_parts + [keys_slot], axis=1).reshape(
            n_slot, extent, local_heads, HEAD_DIM
        )
        values_ext = jnp.concatenate(value_parts + [values_slot], axis=1).reshape(
            n_slot, extent, local_heads, HEAD_DIM
        )
        queries_four = queries.reshape(n_slot, group, local_heads, HEAD_DIM)
        scores = scores_of(queries_four, keys_ext, allowed)
        top = jnp.max(scores, axis=-1, keepdims=True)
        expo = jnp.exp(scores - top)
        summed = jnp.sum(expo, axis=-1, keepdims=True)
        logsum = top + jnp.log(summed)
        probs = (expo / summed).astype(jnp.bfloat16)
        attended = jnp.einsum(
            "shqk,skhd->sqhd", probs, values_ext, preferred_element_type=jnp.float32
        )
        attended = attended.astype(jnp.bfloat16).reshape(rows, head_cols)
        branch_a = lax.psum(plain_dot(attended, full_out), "mp")
        mid = x_in + branch_a
        feed_set = fetch_feed()
        full_gate, full_up, full_down, full_gain_f = feed_set
        gain_f = full_gain_f.astype(jnp.float32)
        normed_f = gain_norm(mid, gain_f).astype(jnp.bfloat16)
        gate_val = plain_dot(normed_f, full_gate)
        up_val = plain_dot(normed_f, full_up)
        hidden_units = gated_unit(gate_val, up_val).astype(jnp.bfloat16)
        branch_f = lax.psum(plain_dot(hidden_units, full_down), "mp")
        result = (mid + branch_f) * valid_rows
        target = teacher[micro].reshape(rows, width).astype(jnp.float32)
        error = (result - target) * valid_rows
        loss_part = loss_part + jnp.sum(error * error)
        results.append(result.astype(jnp.bfloat16).reshape(n_slot, group, width))
        back_feed = fetch_feed()
        full_gate, full_up, full_down, full_gain_f = back_feed
        grad_result = error * factor
        grad_branch = grad_result.astype(jnp.bfloat16)
        acc_down = acc_down + left_dot(hidden_units, grad_branch)
        grad_units = right_dot(grad_branch, full_down)
        unused, pull_unit = jax.vjp(gated_unit, gate_val, up_val)
        grad_gate, grad_upper = pull_unit(grad_units)
        grad_gate = grad_gate.astype(jnp.bfloat16)
        grad_upper = grad_upper.astype(jnp.bfloat16)
        acc_gate = acc_gate + left_dot(normed_f, grad_gate)
        acc_up = acc_up + left_dot(normed_f, grad_upper)
        grad_normed_f = lax.psum(
            right_dot(grad_gate, full_gate) + right_dot(grad_upper, full_up), "mp"
        )
        unused, pull_norm = jax.vjp(gain_norm, mid, gain_f)
        grad_mid_norm, grad_gain_f = pull_norm(grad_normed_f)
        acc_gain_f = acc_gain_f + grad_gain_f
        grad_mid = grad_result + grad_mid_norm
        back_attention = fetch_attention()
        full_query, full_key, full_value, full_out, full_gain_a = back_attention
        grad_att = grad_mid.astype(jnp.bfloat16)
        acc_out = acc_out + left_dot(attended, grad_att)
        grad_attended = (
            right_dot(grad_att, full_out)
            .astype(jnp.bfloat16)
            .reshape(n_slot, group, local_heads, HEAD_DIM)
        )
        scores_again = scores_of(queries_four, keys_ext, allowed)
        probs_back = jnp.exp(scores_again - logsum)
        grad_values_ext = jnp.einsum(
            "shqk,sqhd->skhd",
            probs_back.astype(jnp.bfloat16),
            grad_attended,
            preferred_element_type=jnp.float32,
        )
        grad_probs = jnp.einsum(
            "sqhd,skhd->shqk", grad_attended, values_ext, preferred_element_type=jnp.float32
        )
        inner = jnp.sum(probs_back * grad_probs, axis=-1, keepdims=True)
        grad_scores = (probs_back * (grad_probs - inner)).astype(jnp.bfloat16)
        grad_queries = (
            jnp.einsum("shqk,skhd->sqhd", grad_scores, keys_ext, preferred_element_type=jnp.float32)
            * scale
        )
        grad_keys_ext = (
            jnp.einsum(
                "shqk,sqhd->skhd", grad_scores, queries_four, preferred_element_type=jnp.float32
            )
            * scale
        )
        grad_keys_ext = grad_keys_ext.reshape(n_slot, extent, head_cols)
        grad_values_ext = grad_values_ext.reshape(n_slot, extent, head_cols)
        grad_keys_total = grad_keys_ext[:, reach * group :]
        grad_values_total = grad_values_ext[:, reach * group :]
        for back in range(1, reach + 1):
            offset = (reach - back) * group
            piece_keys = grad_keys_ext[:, offset : offset + group]
            piece_values = grad_values_ext[:, offset : offset + group]
            got_keys, got_values = shifted((piece_keys, piece_values), "ctx", -back)
            grad_keys_total = grad_keys_total + got_keys
            grad_values_total = grad_values_total + got_values
        grad_queries = grad_queries.reshape(rows, head_cols).astype(jnp.bfloat16)
        grad_keys_low = grad_keys_total.reshape(rows, head_cols).astype(jnp.bfloat16)
        grad_values_low = grad_values_total.reshape(rows, head_cols).astype(jnp.bfloat16)
        acc_query = acc_query + left_dot(normed_a, grad_queries)
        acc_key = acc_key + left_dot(normed_a, grad_keys_low)
        acc_value = acc_value + left_dot(normed_a, grad_values_low)
        grad_normed_a = (
            right_dot(grad_queries, full_query)
            + right_dot(grad_keys_low, full_key)
            + right_dot(grad_values_low, full_value)
        )
        grad_normed_a = lax.psum(grad_normed_a, "mp")
        unused, pull_first = jax.vjp(gain_norm, x_in, gain_a)
        grad_x_norm, grad_gain_a = pull_first(grad_normed_a)
        acc_gain_a = acc_gain_a + grad_gain_a
        grad_in = grad_mid + grad_x_norm
        input_grads.append(grad_in.astype(jnp.bfloat16).reshape(n_slot, group, width))
    loss = lax.psum(loss_part, ("dp", "ctx")) / (count * width)
    grads = (
        lax.psum_scatter(acc_query, ("dp", "ctx"), scatter_dimension=0, tiled=True),
        lax.psum_scatter(acc_key, ("dp", "ctx"), scatter_dimension=0, tiled=True),
        lax.psum_scatter(acc_value, ("dp", "ctx"), scatter_dimension=0, tiled=True),
        lax.psum_scatter(acc_out, ("dp", "ctx"), scatter_dimension=1, tiled=True),
        lax.psum_scatter(acc_gate, ("dp", "ctx"), scatter_dimension=0, tiled=True),
        lax.psum_scatter(acc_up, ("dp", "ctx"), scatter_dimension=0, tiled=True),
        lax.psum_scatter(acc_down, ("dp", "ctx"), scatter_dimension=1, tiled=True),
        lax.psum_scatter(acc_gain_a, ("dp", "ctx"), scatter_dimension=0, tiled=True),
        lax.psum_scatter(acc_gain_f, ("dp", "ctx"), scatter_dimension=0, tiled=True),
    )
    return (
        jnp.stack(results),
        loss,
        jnp.stack(input_grads),
        grads[0],
        grads[1],
        grads[2],
        grads[3],
        grads[4],
        grads[5],
        grads[6],
        grads[7],
        grads[8],
    )


def solution(mesh):
    in_specs = (
        P(None, "dp", "ctx", None),
        P(None, "dp", "ctx", None),
        P(),
        P(("dp", "ctx"), "mp"),
        P(("dp", "ctx"), "mp"),
        P(("dp", "ctx"), "mp"),
        P("mp", ("dp", "ctx")),
        P(("dp", "ctx"), "mp"),
        P(("dp", "ctx"), "mp"),
        P("mp", ("dp", "ctx")),
        P(("dp", "ctx")),
        P(("dp", "ctx")),
    )
    out_specs = (
        P(None, "dp", "ctx", None),
        P(),
        P(None, "dp", "ctx", None),
        P(("dp", "ctx"), "mp"),
        P(("dp", "ctx"), "mp"),
        P(("dp", "ctx"), "mp"),
        P("mp", ("dp", "ctx")),
        P(("dp", "ctx"), "mp"),
        P(("dp", "ctx"), "mp"),
        P("mp", ("dp", "ctx")),
        P(("dp", "ctx")),
        P(("dp", "ctx")),
    )
    return jax.shard_map(
        on_device, mesh=mesh, in_specs=in_specs, out_specs=out_specs, check_vma=False
    )
```

profile of v0, /device:TPU:0, one launch (start us, length us, event | category | flops | bytes accessed | tf_op | source)
XLA Modules:
  0.0 3631.6 jit_solution(11140391945610450988)
XLA Ops:
  16.8 22.3 all-gather
  90.2 57.9 %all-gather.12.cloned.1.call-done = bf16[2048,512]{1,0:T(8,128)(2,1)} async-done(((bf16[256,512]{1,0:T(8,128)(2,1)}), bf16[2048,512]{1,0:T(8,128)(2,1)}) %all-gather.12.cloned.1.call-update) | async-done | bytes 2097168 | tf_op jit(solution)/shard_map/all_gather | solution.py:86
  154.3 68.0 %all-gather.10.cloned.1.call-done = bf16[2048,512]{1,0:T(8,128)(2,1)} async-done(((bf16[256,512]{1,0:T(8,128)(2,1)}), bf16[2048,512]{1,0:T(8,128)(2,1)}) %all-gather.10.cloned.1.call-update) | async-done | bytes 2097168 | tf_op jit(solution)/shard_map/all_gather | solution.py:88
  388.4 77.9 %all-gather.1 = bf16[8,1,256]{2,1,0:T(2,128)(2,1)S(1)} all-gather(bf16[1,1,256]{2,1,0:T(2,128)(2,1)S(1)} %reshape.518), channel_id=1, replica_groups=mesh['dp'=2,'ctx'=4,'mp'=4] {'dp','ctx'}, dimensions={0}, use_global_device_ids=true | all-gather | bytes 4608 | tf_op jit(solution)/shard_map/all_gather | solution.py:98
  466.2 269.3 %all-reduce.18.cloned.1.call-done = (f32[1024,2048]{1,0:T(8,128)}, f32[1024,2048]{1,0:T(8,128)}) async-done(((f32[1024,2048]{1,0:T(8,128)}, f32[1024,2048]{1,0:T(8,128)}), (f32[1024,2048]{1,0:T(8,128)}, f32[1024,2048]{1,0:T(8,128)})) %all-reduce.18.cloned.1.call-update) | async-done | bytes 16777232 | tf_op jit(solution)/shard_map/psum | solution.py:162
  758.2 71.2 %all-gather.18.cloned.1.call-done = bf16[2048,1376]{0,1:T(8,128)(2,1)} async-done(((bf16[256,1376]{0,1:T(8,128)(2,1)}), bf16[2048,1376]{0,1:T(8,128)(2,1)}) %all-gather.18.cloned.1.call-update) | async-done | bytes 5636112 | tf_op jit(solution)/shard_map/all_gather | solution.py:95
  848.1 73.5 %all-gather.20.cloned.1.call-done = bf16[2048,1376]{0,1:T(8,128)(2,1)} async-done(((bf16[256,1376]{0,1:T(8,128)(2,1)}), bf16[2048,1376]{0,1:T(8,128)(2,1)}) %all-gather.20.cloned.1.call-update) | async-done | bytes 5636112 | tf_op jit(solution)/shard_map/all_gather | solution.py:96
  942.8 71.1 %all-gather.22.cloned.1.call-done = bf16[1376,2048]{1,0:T(8,128)(2,1)} async-done(((bf16[1376,256]{1,0:T(8,128)(2,1)}), bf16[1376,2048]{1,0:T(8,128)(2,1)}) %all-gather.22.cloned.1.call-update) | async-done | bytes 5636112 | tf_op jit(solution)/shard_map/all_gather | solution.py:97
  1043.6 277.5 %all-reduce.16.cloned.1.call-done = (f32[1024,2048]{1,0:T(8,128)}, f32[1024,2048]{1,0:T(8,128)}) async-done(((f32[1024,2048]{1,0:T(8,128)}, f32[1024,2048]{1,0:T(8,128)}), (f32[1024,2048]{1,0:T(8,128)}, f32[1024,2048]{1,0:T(8,128)})) %all-reduce.16.cloned.1.call-update) | async-done | bytes 16777232 | tf_op jit(solution)/shard_map/psum | solution.py:171
  1321.1 22.2 multiply_reduce_fusion.6
  1417.5 288.3 %all-reduce.14.cloned.1.call-done = (f32[1024,2048]{1,0:T(8,128)}, f32[1024,2048]{1,0:T(8,128)}) async-done(((f32[1024,2048]{1,0:T(8,128)}, f32[1024,2048]{1,0:T(8,128)}), (f32[1024,2048]{1,0:T(8,128)}, f32[1024,2048]{1,0:T(8,128)})) %all-reduce.14.cloned.1.call-update) | async-done | bytes 16777232 | tf_op jit(solution)/shard_map/psum | solution.py:189
  1952.8 55.8 %collective-permute-done.15 = f32[2,512,512]{2,1,0:T(8,128)} collective-permute-done((f32[2,512,512]{2,1,0:T(8,128)}, f32[2,512,512]{2,1,0:T(8,128)}, u32[]{:S(2)}, u32[]{:S(2)}) %collective-permute-start.15) | collective-permute-done | bytes 2097184 | tf_op jit(solution)/shard_map/ppermute | solution.py:18
  2014.6 174.8 %collective-permute-done.13 = f32[2,512,512]{2,1,0:T(8,128)} collective-permute-done((f32[2,512,512]{2,1,0:T(8,128)}, f32[2,512,512]{2,1,0:T(8,128)}, u32[]{:S(2)}, u32[]{:S(2)}) %collective-permute-start.13) | collective-permute-done | bytes 2097184 | tf_op jit(solution)/shard_map/ppermute | solution.py:18
  2192.2 87.0 %collective-permute-done.9 = f32[2,512,512]{2,1,0:T(8,128)} collective-permute-done((f32[2,512,512]{2,1,0:T(8,128)}, f32[2,512,512]{2,1,0:T(8,128)}, u32[]{:S(2)}, u32[]{:S(2)}) %collective-permute-start.9) | collective-permute-done | bytes 2097184 | tf_op jit(solution)/shard_map/ppermute | solution.py:18
  2293.4 74.4 %collective-permute-done.11 = f32[2,512,512]{2,1,0:T(8,128)S(1)} collective-permute-done((f32[2,512,512]{2,1,0:T(8,128)S(1)}, f32[2,512,512]{2,1,0:T(8,128)S(1)}, u32[]{:S(2)}, u32[]{:S(2)}) %collective-permute-start.11) | collective-permute-done | bytes 2097184 | tf_op jit(solution)/shard_map/ppermute | solution.py:18
  2498.0 176.3 %all-reduce.12.cloned.1.call-done = (f32[1024,2048]{1,0:T(8,128)}, f32[1024,2048]{1,0:T(8,128)}) async-done(((f32[1024,2048]{1,0:T(8,128)}, f32[1024,2048]{1,0:T(8,128)}), (f32[1024,2048]{1,0:T(8,128)}, f32[1024,2048]{1,0:T(8,128)})) %all-reduce.12.cloned.1.call-update) | async-done | bytes 16777232 | tf_op jit(solution)/shard_map/psum | solution.py:250
  2691.8 40.1 %all-reduce.2 = (f32[]{:T(128)}, f32[2048]{0:T(1024)S(1)}, f32[2048]{0:T(1024)S(1)}) all-reduce(f32[]{:T(128)S(6)} %add.260, f32[2048]{0:T(1024)S(1)} %add.288, f32[2048]{0:T(1024)S(1)} %add.289), channel_id=1, replica_groups=mesh['dp'=2,'ctx'=4,'mp'=4] {'dp','ctx'}, use_global_device_ids=true, to_apply=%region_14.15 | all-reduce | flops 4097 | bytes 32776 | tf_op jit(solution)/shard_map/psum | solution.py:256
  2733.8 19.3 fusion.14
  2768.1 92.3 %reduce-scatter.8.cloned.1.call-done = f32[256,512]{1,0:T(8,128)} async-done(((f32[2048,512]{1,0:T(8,128)}), f32[256,512]{1,0:T(8,128)}) %reduce-scatter.8.cloned.1.call-update) | async-done | bytes 524304 | tf_op jit(solution)/shard_map/reduce_scatter | solution.py:258
  2860.4 91.8 %reduce-scatter.12.cloned.1.call-done = f32[256,512]{1,0:T(8,128)} async-done(((f32[2048,512]{1,0:T(8,128)}), f32[256,512]{1,0:T(8,128)}) %reduce-scatter.12.cloned.1.call-update) | async-done | bytes 524304 | tf_op jit(solution)/shard_map/reduce_scatter | solution.py:260
  2952.2 92.2 %reduce-scatter.10.cloned.1.call-done = f32[256,512]{1,0:T(8,128)} async-done(((f32[2048,512]{1,0:T(8,128)}), f32[256,512]{1,0:T(8,128)}) %reduce-scatter.10.cloned.1.call-update) | async-done | bytes 524304 | tf_op jit(solution)/shard_map/reduce_scatter | solution.py:259
  3044.4 193.3 %reduce-scatter.20.cloned.1.call-done = f32[1376,256]{1,0:T(8,128)} async-done(((f32[1376,2048]{1,0:T(8,128)}), f32[1376,256]{1,0:T(8,128)}) %reduce-scatter.20.cloned.1.call-update) | async-done | bytes 1409040 | tf_op jit(solution)/shard_map/reduce_scatter | solution.py:264
  3237.7 193.0 %reduce-scatter.18.cloned.1.call-done = f32[256,1376]{0,1:T(8,128)} async-done(((f32[2048,1376]{0,1:T(8,128)}), f32[256,1376]{0,1:T(8,128)}) %reduce-scatter.18.cloned.1.call-update) | async-done | bytes 1409040 | tf_op jit(solution)/shard_map/reduce_scatter | solution.py:263
  3430.7 192.7 %reduce-scatter.16.cloned.1.call-done = f32[256,1376]{0,1:T(8,128)} async-done(((f32[2048,1376]{0,1:T(8,128)}), f32[256,1376]{0,1:T(8,128)}) %reduce-scatter.16.cloned.1.call-update) | async-done | bytes 1409040 | tf_op jit(solution)/shard_map/reduce_scatter | solution.py:262
  (453 shorter events, 828.8 us)
Async XLA Ops:
  8.7 213.6 %all-gather.10.cloned.1.call-start = ((), (), s32[]{:S(2)}) async-start(), calls=%async_computation.7 | async-start | bytes 2359296 | tf_op jit(solution)/shard_map/all_gather | solution.py:88
  9.4 363.0 %all-gather.16.cloned.1.call-start = ((), (), s32[]{:S(2)}) async-start(), calls=%async_computation.10 | async-start | bytes 2359296 | tf_op jit(solution)/shard_map/all_gather | solution.py:89
  10.0 725.5 %all-reduce.18.cloned.1.call-start = ((), (), s32[]{:S(2)}) async-start(), calls=%async_computation.24 | async-start | bytes 33554432 | tf_op jit(solution)/shard_map/psum | solution.py:162
  73.6 203.2 %collective-permute-start.3 = (bf16[2,512,512]{1,2,0:T(8,128)(2,1)}, bf16[2,512,512]{1,2,0:T(8,128)(2,1)}, u32[]{:S(2)}, u32[]{:S(2)}) collective-permute-start(bf16[2,512,512]{1,2,0:T(8,128)(2,1)} %copy.91), channel_id=1, source_target_pairs={{0,4},{4,8},{8,12},{1,5},{5,9},{9,13},{2,6},{6,10},{10,14},{3,7},{... | collective-permute-start | bytes 3145736 | tf_op jit(solution)/shard_map/ppermute | solution.py:18
  84.0 197.4 %collective-permute-start.6 = (bf16[2,512,512]{1,2,0:T(8,128)(2,1)}, bf16[2,512,512]{1,2,0:T(8,128)(2,1)}, u32[]{:S(2)}, u32[]{:S(2)}) collective-permute-start(bf16[2,512,512]{1,2,0:T(8,128)(2,1)} %copy.101), channel_id=1, source_target_pairs={{0,8},{4,12},{1,9},{5,13},{2,10},{6,14},{3,11},{7,15},{16,24},{20,... | collective-permute-start | bytes 3145736 | tf_op jit(solution)/shard_map/ppermute | solution.py:18
  86.3 200.1 %collective-permute-start.7 = (bf16[2,512,512]{1,2,0:T(8,128)(2,1)}, bf16[2,512,512]{1,2,0:T(8,128)(2,1)}, u32[]{:S(2)}, u32[]{:S(2)}) collective-permute-start(bf16[2,512,512]{1,2,0:T(8,128)(2,1)} %copy.101), channel_id=1, source_target_pairs={{0,4},{4,8},{8,12},{1,5},{5,9},{9,13},{2,6},{6,10},{10,14},{3,7},{... | collective-permute-start | bytes 3145736 | tf_op jit(solution)/shard_map/ppermute | solution.py:18
  386.2 443.2 %all-gather.18.cloned.1.call-start = ((), (), s32[]{:S(2)}) async-start(), calls=%async_computation.11 | async-start | bytes 6340608 | tf_op jit(solution)/shard_map/all_gather | solution.py:95
  386.8 534.8 %all-gather.20.cloned.1.call-start = ((), (), s32[]{:S(2)}) async-start(), calls=%async_computation.12 | async-start | bytes 6340608 | tf_op jit(solution)/shard_map/all_gather | solution.py:96
  387.5 626.3 %all-gather.22.cloned.1.call-start = ((), (), s32[]{:S(2)}) async-start(), calls=%async_computation.13 | async-start | bytes 6340608 | tf_op jit(solution)/shard_map/all_gather | solution.py:97
  388.3 932.8 %all-reduce.16.cloned.1.call-start = ((), (), s32[]{:S(2)}) async-start(), calls=%async_computation.23 | async-start | bytes 33554432 | tf_op jit(solution)/shard_map/psum | solution.py:171
  1033.9 671.9 %all-reduce.14.cloned.1.call-start = ((), (), s32[]{:S(2)}) async-start(), calls=%async_computation.22 | async-start | bytes 33554432 | tf_op jit(solution)/shard_map/psum | solution.py:189
  1416.8 1257.6 %all-reduce.12.cloned.1.call-start = ((), (), s32[]{:S(2)}) async-start(), calls=%async_computation.21 | async-start | bytes 33554432 | tf_op jit(solution)/shard_map/psum | solution.py:250
  1907.0 282.4 %collective-permute-start.13 = (f32[2,512,512]{2,1,0:T(8,128)}, f32[2,512,512]{2,1,0:T(8,128)}, u32[]{:S(2)}, u32[]{:S(2)}) collective-permute-start(f32[2,512,512]{2,1,0:T(8,128)} %copy.144), channel_id=1, source_target_pairs={{8,0},{12,4},{9,1},{13,5},{10,2},{14,6},{11,3},{15,7},{24,16},{28,... | collective-permute-start | bytes 6291464 | tf_op jit(solution)/shard_map/ppermute | solution.py:18
  1919.0 273.2 %collective-permute-start.8 = (f32[2,512,512]{2,1,0:T(8,128)}, f32[2,512,512]{2,1,0:T(8,128)}, u32[]{:S(2)}, u32[]{:S(2)}) collective-permute-start(f32[2,512,512]{2,1,0:T(8,128)} %copy.137), channel_id=1, source_target_pairs={{4,0},{8,4},{12,8},{5,1},{9,5},{13,9},{6,2},{10,6},{14,10},{7,3},{... | collective-permute-start | bytes 6291464 | tf_op jit(solution)/shard_map/ppermute | solution.py:18
  1922.2 357.1 %collective-permute-start.9 = (f32[2,512,512]{2,1,0:T(8,128)}, f32[2,512,512]{2,1,0:T(8,128)}, u32[]{:S(2)}, u32[]{:S(2)}) collective-permute-start(f32[2,512,512]{2,1,0:T(8,128)} %copy.138), channel_id=1, source_target_pairs={{8,0},{12,4},{9,1},{13,5},{10,2},{14,6},{11,3},{15,7},{24,16},{28,... | collective-permute-start | bytes 6291464 | tf_op jit(solution)/shard_map/ppermute | solution.py:18
  2008.7 284.8 %collective-permute-start.10 = (f32[2,512,512]{2,1,0:T(8,128)S(1)}, f32[2,512,512]{2,1,0:T(8,128)S(1)}, u32[]{:S(2)}, u32[]{:S(2)}) collective-permute-start(f32[2,512,512]{2,1,0:T(8,128)S(1)} %copy-done.46), channel_id=1, source_target_pairs={{4,0},{8,4},{12,8},{5,1},{9,5},{13,9},{6,2},{10,6},{14,10},{7,3},{... | collective-permute-start | bytes 6291464 | tf_op jit(solution)/shard_map/ppermute | solution.py:18
  2010.0 357.9 %collective-permute-start.11 = (f32[2,512,512]{2,1,0:T(8,128)S(1)}, f32[2,512,512]{2,1,0:T(8,128)S(1)}, u32[]{:S(2)}, u32[]{:S(2)}) collective-permute-start(f32[2,512,512]{2,1,0:T(8,128)S(1)} %copy-done.45), channel_id=1, source_target_pairs={{8,0},{12,4},{9,1},{13,5},{10,2},{14,6},{11,3},{15,7},{24,16},{28,... | collective-permute-start | bytes 6291464 | tf_op jit(solution)/shard_map/ppermute | solution.py:18
  2387.9 380.2 %reduce-scatter.14.cloned.1.call-start = ((), (), s32[]{:S(2)}) async-start(), calls=%async_computation.17 | async-start | bytes 4718592 | tf_op jit(solution)/shard_map/reduce_scatter | solution.py:261
  2404.1 456.3 %reduce-scatter.8.cloned.1.call-start = ((), (), s32[]{:S(2)}) async-start(), calls=%async_computation.14 | async-start | bytes 4718592 | tf_op jit(solution)/shard_map/reduce_scatter | solution.py:258
  2417.1 535.1 %reduce-scatter.12.cloned.1.call-start = ((), (), s32[]{:S(2)}) async-start(), calls=%async_computation.16 | async-start | bytes 4718592 | tf_op jit(solution)/shard_map/reduce_scatter | solution.py:260
  2426.8 617.6 %reduce-scatter.10.cloned.1.call-start = ((), (), s32[]{:S(2)}) async-start(), calls=%async_computation.15 | async-start | bytes 4718592 | tf_op jit(solution)/shard_map/reduce_scatter | solution.py:259
  2436.6 801.1 %reduce-scatter.20.cloned.1.call-start = ((), (), s32[]{:S(2)}) async-start(), calls=%async_computation.20 | async-start | bytes 12681216 | tf_op jit(solution)/shard_map/reduce_scatter | solution.py:264
  2459.2 971.5 %reduce-scatter.18.cloned.1.call-start = ((), (), s32[]{:S(2)}) async-start(), calls=%async_computation.19 | async-start | bytes 12681216 | tf_op jit(solution)/shard_map/reduce_scatter | solution.py:263
  2476.8 1146.5 %reduce-scatter.16.cloned.1.call-start = ((), (), s32[]{:S(2)}) async-start(), calls=%async_computation.18 | async-start | bytes 12681216 | tf_op jit(solution)/shard_map/reduce_scatter | solution.py:262
  (125 other events, 4948.3 us)
Sparse Core Ops, SparseCore 0:
  10.1 52.1 all-gather.13
  64.5 83.5 all-gather.11
  150.3 72.0 all-gather.9
  224.2 89.1 all-gather.15
  386.3 349.1 all-reduce.17
  737.3 92.0 all-gather.17
  831.4 90.1 all-gather.19
  923.6 90.1 all-gather.21
  1034.0 287.0 all-reduce.15
  1416.9 288.8 all-reduce.13
  2388.1 286.2 all-reduce.11
  2678.4 89.6 reduce-scatter.13
  2772.8 87.6 reduce-scatter.7
  2864.5 87.6 reduce-scatter.11
  2956.7 87.6 reduce-scatter.9
  3048.5 189.1 reduce-scatter.19
  3242.3 188.3 reduce-scatter.17
  3434.8 188.5 reduce-scatter.15
where the time goes:
time: 3640 us; the launch traced here: 3630 us
  waiting for transfers between devices  2630 us (72%)
  matrix products  460 us (13%)
  other arithmetic  209 us (6%)
  blocking collectives  140 us (4%)
  local copies, waits for them, and re-layouts  121 us (3%)
  starting transfers between devices  54.3 us (1%)
    ppermute x16, waiting for transfers between devices, shifted(): lax.ppermute(value, axis, [(source, source + steps) for source in range(l...  392 us
    psum x1, waiting for transfers between devices, on_device(): lax.psum(right_dot(grad_gate, full_gate) + right_dot(grad_upper, full_up)...  288 us
    psum x1, waiting for transfers between devices, on_device(): branch_f = lax.psum(plain_dot(hidden_units, full_down), 'mp')  277 us
    psum x1, waiting for transfers between devices, on_device(): branch_a = lax.psum(plain_dot(attended, full_out), 'mp')  269 us
    reduce_scatter x1, waiting for transfers between devices, on_device(): lax.psum_scatter(acc_down, ('dp', 'ctx'), scatter_dimension=1, tiled=True)  193 us
    reduce_scatter x1, waiting for transfers between devices, on_device(): lax.psum_scatter(acc_up, ('dp', 'ctx'), scatter_dimension=0, tiled=True)  193 us
    reduce_scatter x1, waiting for transfers between devices, on_device(): lax.psum_scatter(acc_gate, ('dp', 'ctx'), scatter_dimension=0, tiled=True)  193 us
    psum x1, waiting for transfers between devices, on_device(): grad_normed_a = lax.psum(grad_normed_a, 'mp')  176 us
  transfers between devices with their start and end apart: 34, of which 21 were waited for; matrix products, arithmetic and copies ran while one was open for 14% of the time, Pallas kernels for 0%

commit v1 on v0

--- a/solution.py
+++ b/solution.py
@@ -1,15 +1,676 @@
 import jax
 import jax.numpy as jnp
 from jax import lax
+from jax.experimental import pallas as pl
+from jax.experimental.pallas import tpu as pltpu
 from jax.sharding import PartitionSpec as P
 
 HEAD_DIM = 128
 WINDOW = 1024
 SEQ = 2048
-
-
 EPS = 1e-06
 NEGATIVE = -1e30
+BF = jnp.bfloat16
+F32 = jnp.float32
+
+
+def dot_t(a, b, dims):
+    return lax.dot_general(a, b, (dims, ((), ())), preferred_element_type=F32)
+
+
+def plain_dot(left, right):
+    return dot_t(left, right, ((1,), (0,)))
+
+
+def left_dot(left, right):
+    return dot_t(left, right, ((0,), (0,)))
+
+
+def right_dot(left, right):
+    return dot_t(left, right, ((1,), (1,)))
+
+
+def masked_scores(q, k, behind, length, kcol, qrow, kbase):
+    s = right_dot(k, q) * (HEAD_DIM**-0.5)
+    valid = kcol + kbase < length
+    if behind == 0:
+        keep = (qrow >= jnp.where(valid, kcol, SEQ)) | (qrow == kcol)
+    elif behind == 1:
+        keep = jnp.broadcast_to(valid, s.shape)
+    else:
+        keep = qrow < jnp.where(valid, kcol, -1)
+    return jnp.where(keep, s, NEGATIVE)
+
+
+def piece(ref, block, rows):
+    return ref[block * rows : (block + 1) * rows, :]
+
+
+def attend_kernel(pair, per, back, len_ref, kcol_ref, qrow_ref, q_ref, *refs):
+    n = (len(refs) - 2) // 2
+    k_refs, v_refs, (o_ref, lse_ref) = refs[:n], refs[n : 2 * n], refs[2 * n :]
+    rows = kcol_ref.shape[0]
+    length = len_ref[0]
+    kcol, qrow = kcol_ref[...], qrow_ref[...]
+    base = (pair - n + 1) * per
+    for b in range(per):
+        chunk = pair * per + b
+        seen = range(max(0, chunk - back), chunk + 1)
+        where = [divmod(j - base, per) for j in seen]
+        q = piece(q_ref, b, rows)
+        scores = [
+            masked_scores(q, piece(k_refs[p], i, rows), chunk - j, length, kcol, qrow, j * rows)
+            for j, (p, i) in zip(seen, where)
+        ]
+        top = jnp.max(scores[0], axis=0, keepdims=True)
+        for s in scores[1:]:
+            top = jnp.maximum(top, jnp.max(s, axis=0, keepdims=True))
+        expo = [jnp.exp(s - top) for s in scores]
+        total = jnp.sum(expo[0], axis=0, keepdims=True)
+        for e in expo[1:]:
+            total = total + jnp.sum(e, axis=0, keepdims=True)
+        inv = 1.0 / total
+        out = jnp.zeros((HEAD_DIM, rows), F32)
+        for e, (p, i) in zip(expo, where):
+            out = out + left_dot(piece(v_refs[p], i, rows), (e * inv).astype(BF))
+        o_ref[b * rows : (b + 1) * rows, :] = out.T.astype(BF)
+        lse_ref[0, b : b + 1, :] = top + jnp.log(total)
+
+
+def attend_back_kernel(pair, per, back, len_ref, kcol_ref, qrow_ref, q_ref, g_ref, lse_ref, *refs):
+    n = (len(refs) - 1 + 2) // 6
+    k_refs, v_refs = refs[:n], refs[n : 2 * n]
+    in_refs = refs[2 * n : 4 * n - 2]
+    gq_ref, out_refs = refs[4 * n - 2], refs[4 * n - 1 :]
+    rows = kcol_ref.shape[0]
+    length = len_ref[0]
+    kcol, qrow = kcol_ref[...], qrow_ref[...]
+    scale = HEAD_DIM**-0.5
+    base = (pair - n + 1) * per
+    sums = {}
+    for b in range(per):
+        chunk = pair * per + b
+        seen = range(max(0, chunk - back), chunk + 1)
+        where = [divmod(j - base, per) for j in seen]
+        q, g = piece(q_ref, b, rows), piece(g_ref, b, rows)
+        lse = lse_ref[0, b : b + 1, :]
+        probs, gprobs = [], []
+        inner = jnp.zeros((1, rows), F32)
+        for j, (p, i) in zip(seen, where):
+            s = masked_scores(q, piece(k_refs[p], i, rows), chunk - j, length, kcol, qrow, j * rows)
+            e = jnp.exp(s - lse)
+            ge = right_dot(piece(v_refs[p], i, rows), g)
+            inner = inner + jnp.sum(e * ge, axis=0, keepdims=True)
+            probs.append(e)
+            gprobs.append(ge)
+        gq = jnp.zeros((HEAD_DIM, rows), F32)
+        for e, ge, at in zip(probs, gprobs, where):
+            gs = (e * (ge - inner)).astype(BF)
+            gq = gq + left_dot(piece(k_refs[at[0]], at[1], rows), gs)
+            gk, gv = plain_dot(gs, q) * scale, plain_dot(e.astype(BF), g)
+            if at in sums:
+                gk, gv = gk + sums[at][0], gv + sums[at][1]
+            sums[at] = (gk, gv)
+        gq_ref[b * rows : (b + 1) * rows, :] = (gq.T * scale).astype(BF)
+    for p in range(n):
+        for i in range(per):
+            at = slice(i * rows, (i + 1) * rows)
+            for which in range(2):
+                out_ref = out_refs[which * n + p]
+                value = sums[p, i][which] if (p, i) in sums else None
+                if p < n - 1:
+                    before = in_refs[which * (n - 1) + p][at, :]
+                    value = before if value is None else value + before
+                out_ref[at, :] = value.astype(out_ref.dtype)
+
+
+def attend_call(kernel, name, pair, per, back, kcol, qrow, length, ins, lses, shapes, n_dots):
+    rows = kcol.shape[0]
+    wide, cols = ins[0].shape
+    heads = cols // HEAD_DIM
+    block = pl.BlockSpec((wide, HEAD_DIM), lambda h, *_: (0, h))
+    lse_block = pl.BlockSpec((1, per, rows), lambda h, *_: (h, 0, 0))
+    blocks = sum(min(pair * per + b, back) + 1 for b in range(per))
+    n_lse = len(lses)
+    return pl.pallas_call(
+        lambda *refs: kernel(pair, per, back, *refs),
+        grid_spec=pltpu.PrefetchScalarGridSpec(
+            num_scalar_prefetch=1,
+            grid=(heads,),
+            in_specs=[
+                pl.BlockSpec((rows, 1), lambda h, *_: (0, 0)),
+                pl.BlockSpec((1, rows), lambda h, *_: (0, 0)),
+            ]
+            + ([block] * 2 + [lse_block] + [block] * (len(ins) - 2) if lses else [block] * len(ins)),
+            out_specs=[block if shape.ndim == 2 else lse_block for shape in shapes],
+        ),
+        out_shape=shapes,
+        compiler_params=pltpu.CompilerParams(vmem_limit_bytes=56 << 20),
+        cost_estimate=pl.CostEstimate(
+            flops=6 * n_dots * blocks * rows * rows * HEAD_DIM * heads,
+            bytes_accessed=2 * wide * cols * (len(ins) + len(shapes)),
+            transcendentals=blocks * rows * rows * heads,
+        ),
+        name=f"{name}{pair}",
+    )(length, kcol, qrow, *((*ins[:2], *lses, *ins[2:]) if lses else ins))
+
+
+def core_swap(v):
+    return lax.ppermute(v, "mp", [(i, i ^ 1) for i in range(4)])
+
+
+def chip_swap(v):
+    return lax.ppermute(v, "mp", [(i, i ^ 2) for i in range(4)])
+
+
+def dp_swap(v):
+    return lax.ppermute(v, "dp", [(i, i ^ 1) for i in range(2)])
+
+
+def ctx_turn(v, steps):
+    n = lax.axis_size("ctx")
+    return lax.ppermute(v, "ctx", [(i, (i + steps) % n) for i in range(n)])
+
+
+def after(value, *others):
+    return lax.optimization_barrier((value, *others))[0]
+
+
+def pick(v, index):
+    return lax.dynamic_index_in_dim(v, index, 0, keepdims=False)
+
+
+def join(got, own):
+    return jnp.concatenate([own, got], axis=1)
+
+
+def join_flat(got, own):
+    return join(got, own).reshape(-1, own.shape[2])
+
+
+class Order:
+    def __init__(self):
+        self.last = ()
+
+    def __call__(self, step, first, *rest):
+        if self.last:
+            first = after(first, *self.last)
+        out = step(first, *rest)
+        self.last = (jax.tree.leaves(out)[0],)
+        return out
+
+    def wait(self, *values):
+        self.last = (*self.last, *values)
+
+
+def split_part(part, per):
+    part = part.reshape(per, -1, part.shape[1])
+    return part[:, part.shape[1] // 2 :].astype(BF), part
+
+
+def add_core(got, keep):
+    mine = keep[:, : keep.shape[1] // 2] + got.astype(F32)
+    half = mine.shape[1] // 2
+    return mine[:, half:].astype(BF), mine[:, :half]
+
+
+def own_first(v, y):
+    half = v.shape[-1] // 2
+    return jnp.where(y == 0, v, jnp.concatenate([v[..., half:], v[..., :half]], axis=-1))
+
+
+def whole_part(right, left):
+    return left_dot(left, right)
+
+
+def whole_rest(right, left, part):
+    return (part + left_dot(left, right)).astype(BF)
+
+
+def their_part(right, left):
+    return left_dot(left[:, left.shape[1] // 2 :], right)
+
+
+def their_rest(right, left, part):
+    return (part + their_part(right, left)).astype(BF)
+
+
+def own_part_grad(right, left):
+    return left_dot(left[:, : left.shape[1] // 2], right)
+
+
+def own_rest(right, left, part, got):
+    return (part + own_part_grad(right, left) + got.astype(F32)).astype(BF)
+
+
+def both_scatter(grad):
+    halves = grad.reshape(2, -1, grad.shape[1])
+    return lax.psum_scatter(halves, "ctx", scatter_dimension=1, tiled=True)
+
+
+def ring_scatter(grad, z):
+    n = lax.axis_size("ctx")
+    blocks = grad.reshape(n, -1, grad.shape[1])
+    travel = pick(blocks, (z + n - 1) % n)
+    for k in range(2, n + 1):
+        total = pick(blocks, (z + n - k) % n).astype(F32) + ctx_turn(travel, 1).astype(F32)
+        travel = total.astype(BF)
+    return total
+
+
+def to_slots(v, z):
+    n = v.shape[0]
+    return [pick(v, z)] + [ctx_turn(pick(v, (z + k) % n), k) for k in range(1, n)]
+
+
+def place_kernel(index_ref, *refs):
+    step = pl.program_id(0)
+    for i, ref in enumerate(refs[:-1]):
+
+        @pl.when(step == i)
+        def _(ref=ref):
+            refs[-1][0, 0] = ref[...]
+
+
+def whole_rows(blocks, index, n):
+    rows, width = blocks[0].shape
+    return pl.pallas_call(
+        place_kernel,
+        grid_spec=pltpu.PrefetchScalarGridSpec(
+            num_scalar_prefetch=1,
+            grid=(len(blocks),),
+            in_specs=[
+                pl.BlockSpec((rows, width), lambda i, _: (0, 0), pipeline_mode=pl.Buffered(1))
+            ]
+            * len(blocks),
+            out_specs=pl.BlockSpec((1, 1, rows, width), lambda i, at: (at[i, 0], at[i, 1], 0, 0)),
+        ),
+        out_shape=jax.ShapeDtypeStruct((n, 4, rows, width), blocks[0].dtype),
+        compiler_params=pltpu.CompilerParams(vmem_limit_bytes=24 << 20),
+        cost_estimate=pl.CostEstimate(
+            flops=0, bytes_accessed=4 * len(blocks) * rows * width, transcendentals=0
+        ),
+        name="place_rows",
+    )(jnp.stack([jnp.stack(at) for at in index]).astype(jnp.int32), *blocks)
+
+
+def all_sum(v):
+    v = v + core_swap(v)
+    v = v + chip_swap(v)
+    v = v + dp_swap(v)
+    n = lax.axis_size("ctx")
+    step = 1
+    while step < n:
+        v = v + lax.ppermute(v, "ctx", [(i, i ^ step) for i in range(n)])
+        step *= 2
+    return v
+
+
+def norm_scale(v):
+    return lax.rsqrt(jnp.mean(v * v, axis=-1, keepdims=True) + EPS)
+
+
+def norm_back(v, r, gain, grad):
+    z = v * r
+    e = grad * gain
+    return r * (e - z * jnp.mean(e * z, axis=-1, keepdims=True)), jnp.sum(grad * z, axis=(0, 1))
+
+
+def slot_device(
+    hidden_in,
+    teacher,
+    lengths,
+    query_weight,
+    key_weight,
+    value_weight,
+    out_weight,
+    gate_weight,
+    up_weight,
+    down_weight,
+    attention_gain,
+    feed_gain,
+):
+    n_micro, n_slot, group, width = hidden_in.shape
+    n_chunk = n_micro * n_slot
+    quarter = group // 4
+    cols = query_weight.shape[1]
+    heads = cols // HEAD_DIM
+    back = WINDOW // group
+    ctx_index = lax.axis_index("ctx")
+    dp_index = lax.axis_index("dp")
+    mp_index = lax.axis_index("mp")
+    core_index, x_index = mp_index % 2, mp_index // 2
+    place = core_index * 2 + x_index
+    share = attention_gain.shape[0]
+    count = jnp.sum(lengths).astype(F32)
+    factor = lengths.shape[0] * lengths.shape[1] * SEQ / count
+    length = lax.dynamic_slice(
+        lengths, (ctx_index // n_slot, dp_index * n_slot + ctx_index % n_slot), (1, 1)
+    ).reshape(1)
+    row = jnp.arange(group, dtype=jnp.int32)
+    inside = ((row // quarter) ^ place) * quarter + row % quarter
+    kcol, qrow = inside[:, None], inside[None, :]
+    own_inside = place * quarter + jnp.arange(quarter, dtype=jnp.int32)
+    chunks = range(n_chunk)
+
+    def own_part(v):
+        v = lax.dynamic_slice_in_dim(v.reshape(n_chunk, group, width), place * quarter, quarter, 1)
+        return to_slots(own_first(v, dp_index), ctx_index)
+
+    def by_chunk(parts):
+        parts = jnp.stack(parts)
+        return [pick(parts, (ctx_index - c) % n_chunk) for c in chunks]
+
+    x_parts = own_part(hidden_in)
+    x_peers = [chip_swap(part) for part in x_parts]
+    x_pairs = [jnp.concatenate(pair, axis=0) for pair in zip(x_parts, x_peers)]
+    x_cores = [core_swap(pair) for pair in x_pairs]
+    x_own = by_chunk(x_parts)
+    x_all = by_chunk([jnp.concatenate(pair, axis=0) for pair in zip(x_pairs, x_cores)])
+    gain_rows = jnp.pad(jnp.stack([attention_gain, feed_gain]), ((0, 14), (0, cols - share)))
+    shards = [
+        jnp.concatenate([query_weight, gain_rows], axis=0),
+        key_weight,
+        value_weight,
+        out_weight.T,
+        gate_weight,
+        up_weight,
+    ]
+    parts = []
+    for i, shard in enumerate(shards):
+        if i > 0:
+            shard = after(shard, *x_parts, *parts[-2:-1])
+        parts.append(lax.all_gather(shard, "ctx", axis=0, tiled=True))
+    shard = after(down_weight.T, *x_parts, *parts[-2:-1])
+    part_down = [
+        lax.all_gather(v, "ctx", axis=0, tiled=True) for v in (shard, dp_swap(down_weight.T))
+    ]
+    w_down = jnp.concatenate(part_down, axis=0)
+    gates = [x_parts, x_peers, x_cores] + [()] * 3
+    fetched = [(part, dp_swap(after(part, *gate))) for part, gate in zip(parts, gates)]
+    query_parts = [part.reshape(n_chunk, share + 16, cols) for part in fetched[0]]
+    fetched[0] = [part[:, :share].reshape(n_chunk * share, cols) for part in query_parts]
+    gain_a, gain_f = [
+        jnp.concatenate([part[:, share + i, :share].reshape(-1) for part in query_parts]).astype(F32)
+        for i in range(2)
+    ]
+    part_gate, part_up = parts[4:]
+    w_query, w_key, w_value, w_out, w_gate, w_up = [
+        jnp.concatenate(pair, axis=0) for pair in fetched
+    ]
+    teacher_parts = own_part(after(teacher, part_up))
+    target = by_chunk(teacher_parts)
+    per = 2
+    pairs = range(n_chunk // per)
+    x_own = [jnp.stack(x_own[p * per : (p + 1) * per]) for p in pairs]
+    target = [jnp.stack(target[p * per : (p + 1) * per]) for p in pairs]
+    order = Order()
+    reach = -(-back // per)
+    mid, r_f, sent, kept = [], [], {}, {}
+
+    def gather_half(own):
+        return order(join, chip_swap(own), own)
+
+    def gather_rest(pair):
+        return order(join_flat, core_swap(pair), pair)
+
+    def pass_core(p):
+        sent[p], kept[p] = order(add_core, core_swap(sent[p]), kept[p])
+
+    h1, queries, keys, values, attended, lse, h2 = [], [], [], [], [], [], []
+
+    def project(h):
+        return [plain_dot(h, w).astype(BF) for w in (w_query, w_key, w_value)]
+
+    def normed(*xs):
+        x = jnp.concatenate(xs, axis=0).astype(F32)
+        return (x * norm_scale(x) * gain_a).astype(BF)
+
+    def attention(p):
+        first = max(0, p - reach)
+
+        def step(q):
+            ins = [q, *keys[first : p + 1], *values[first : p + 1]]
+            shapes = [
+                jax.ShapeDtypeStruct(q.shape, BF),
+                jax.ShapeDtypeStruct((heads, per, group), F32),
+            ]
+            return attend_call(
+                attend_kernel, "attend", p, per, back, kcol, qrow, length, ins, [], shapes, 4
+            )
+
+        a, l = order(step, queries[p])
+        attended.append(a)
+        lse.append(l)
+
+    def enter_feed(p):
+        def step(got, keep, x):
+            v = x.astype(F32) + (keep + got.astype(F32))
+            r = norm_scale(v)
+            return (v * r * gain_f).astype(BF), v, r
+
+        low, v, r = order(step, chip_swap(sent[p]), kept[p], x_own[p])
+        mid.append(v)
+        r_f.append(r)
+        return low
+
+    for p in pairs:
+        h1.append(order(normed, *x_all[p * per : (p + 1) * per]))
+    for p in pairs:
+        q, k, v = order(project, h1[p])
+        queries.append(q)
+        keys.append(k)
+        values.append(v)
+        order.wait((parts[3], part_gate)[p])
+        attention(p)
+        sent[p], kept[p] = order(lambda a: split_part(right_dot(a, w_out), per), attended[p])
+    pass_core(0)
+    pass_core(1)
+    low = [enter_feed(0)]
+    order.wait(part_up, fetched[4][1])
+    low.append(enter_feed(1))
+    low[0] = gather_half(low[0])
+    order.wait(fetched[5][1])
+    low[1] = gather_half(low[1])
+    h2 += [gather_rest(v) for v in low]
+
+    gate, up, hidden, results, g_result, g_branch, loss_parts = [], [], [], [], [], [], []
+
+    def unit(h):
+        g, u = plain_dot(h, w_gate), plain_dot(h, w_up)
+        return (g * jax.nn.sigmoid(g) * u).astype(BF), g, u
+
+    def finish(p):
+        def step(got, keep, v, t):
+            at = (p * per + jnp.arange(per, dtype=jnp.int32))[:, None] * group + own_inside
+            valid = (at < length)[:, :, None].astype(F32)
+            result = (v + (keep + got.astype(F32))) * valid
+            error = (result - t.astype(F32)) * valid
+            grad = error * factor
+            return grad.astype(BF), grad, result.astype(BF), jnp.sum(error * error)
+
+        low, grad, result, loss = order(step, chip_swap(sent[p]), kept[p], mid[p], target[p])
+        results.append(result)
+        g_result.append(grad)
+        loss_parts.append(loss)
+        return low
+
+    for p in pairs:
+        h, g, u = order(unit, h2[p])
+        hidden.append(h)
+        gate.append(g)
+        up.append(u)
+        if p == 0:
+            order.wait(*teacher_parts)
+    for p in pairs:
+        sent[p], kept[p] = order(lambda h: split_part(right_dot(h, w_down), per), hidden[p])
+    pass_core(0)
+    pass_core(1)
+    low = [finish(0), finish(1)]
+    low[0] = gather_half(low[0])
+    g_branch.append(gather_rest(low[0]))
+
+    g_gate, g_up, g_mid, g_att, gain_f_parts = [], [], [], [], []
+
+    def leave_unit(p):
+        def step(g_out, g, u):
+            g_hidden = plain_dot(g_out, w_down)
+            sig = jax.nn.sigmoid(g)
+            return (
+                (g_hidden * g * sig).astype(BF),
+                (g_hidden * u * sig * (1.0 + g * (1.0 - sig))).astype(BF),
+            )
+
+        gu, gg = order(step, g_branch[p], gate[p], up[p])
+        g_up.append(gu)
+        g_gate.append(gg)
+
+    def project_unit(p):
+        def step(gg, gu):
+            return split_part(right_dot(gg, w_gate) + right_dot(gu, w_up), per)
+
+        sent[p], kept[p] = order(step, g_gate[p], g_up[p])
+
+    def enter_attention(p):
+        def step(got, keep, v, r, grad):
+            g_norm, g_gain = norm_back(v, r, gain_f, keep + got.astype(F32))
+            total = grad + g_norm
+            return total.astype(BF), total, g_gain
+
+        low, total, g_gain = order(step, chip_swap(sent[p]), kept[p], mid[p], r_f[p], g_result[p])
+        g_mid.append(total)
+        gain_f_parts.append(g_gain)
+        return low
+
+    scattered = []
+
+    def scatter(rights, lefts, got):
+        part = order(own_part_grad, rights[0], lefts[0])
+        own = order(own_rest, rights[1], lefts[1], part, got)
+        scattered.append(ring_scatter(own, ctx_index))
+
+    def send(rights, lefts):
+        part = order(their_part, rights[0], lefts[0])
+        return dp_swap(order(their_rest, rights[1], lefts[1], part))
+
+    part = order(whole_part, hidden[0], g_branch[0])
+    leave_unit(0)
+    low[1] = gather_half(low[1])
+    gate_part = order(whole_part, g_gate[0], h2[0])
+    g_branch.append(gather_rest(low[1]))
+    d_down = order(whole_rest, hidden[1], g_branch[1], part)
+    s_down = both_scatter(d_down)
+    leave_unit(1)
+    s_gate = both_scatter(order(whole_rest, g_gate[1], h2[1], gate_part))
+    up_part = order(whole_part, g_up[0], h2[0])
+    s_up = both_scatter(order(whole_rest, g_up[1], h2[1], up_part))
+    project_unit(0)
+    pass_core(0)
+    project_unit(1)
+    pass_core(1)
+    low = [enter_attention(0), enter_attention(1)]
+    low[0] = gather_half(low[0])
+    g_att.append(gather_rest(low[0]))
+
+    g_q, g_k, g_v = [None] * len(pairs), [None] * len(pairs), [None] * len(pairs)
+    g_in, gain_a_parts = [], []
+
+    def attention_back(p):
+        first = max(0, p - reach)
+        last = p == len(pairs) - 1
+
+        def step(g):
+            ins = [queries[p], plain_dot(g, w_out).astype(BF), *keys[first : p + 1], *values[first : p + 1]]
+            kinds = [BF if last or p - j == reach else F32 for j in range(first, p + 1)]
+            shape = ins[0].shape
+            shapes = [jax.ShapeDtypeStruct(shape, kind) for kind in [BF] + kinds * 2]
+            return attend_call(
+                attend_back_kernel, "attend_back", p, per, back, kcol, qrow, length,
+                [*ins, *g_k[first:p], *g_v[first:p]], [lse[p]], shapes, 10,
+            )
+
+        out = order(step, g_att[p])
+        n = p - first + 1
+        g_q[p] = out[0]
+        g_k[first : p + 1] = out[1 : 1 + n]
+        g_v[first : p + 1] = out[1 + n :]
+
+    def project_back(p):
+        def step(q, k, v):
+            whole = right_dot(q, w_query) + right_dot(k, w_key) + right_dot(v, w_value)
+            return split_part(whole, per)
+
+        sent[p], kept[p] = order(step, g_q[p], g_k[p], g_v[p])
+
+    def leave(p):
+        def step(got, keep, x, grad):
+            x = x.astype(F32)
+            g_norm, g_gain = norm_back(x, norm_scale(x), gain_a, keep + got.astype(F32))
+            return (grad + g_norm).astype(BF), g_gain
+
+        low, g_gain = order(step, chip_swap(sent[p]), kept[p], x_own[p], g_mid[p])
+        g_in.append(low)
+        gain_a_parts.append(g_gain)
+
+    attention_back(0)
+    low[1] = gather_half(low[1])
+    g_att.append(gather_rest(low[1]))
+    results = [after(v, low[1]) for v in results]
+    out_parts = to_slots(own_first(jnp.concatenate(results, axis=0), dp_index), ctx_index)
+    out_got = send(attended, g_att)
+    attention_back(1)
+    order.wait(s_gate)
+    project_back(0)
+    project_back(1)
+    out_own = order(lambda first, *rest: jnp.stack([first, *rest]), *out_parts)
+    out_peer, out_core = chip_swap(out_own), core_swap(out_own)
+    pass_core(0)
+    got = [send(g_q, h1)]
+    pass_core(1)
+    got += [send(right, h1) for right in (g_k, g_v)]
+    leave(0)
+    leave(1)
+    back_parts = to_slots(own_first(jnp.concatenate(g_in, axis=0), dp_index), ctx_index)
+    scatter(attended, g_att, out_got)
+    slots = [(ctx_index - k) % n_chunk for k in chunks]
+    index = [(slot, place ^ i) for slot in slots for i in range(4)]
+
+    def place_out(own, *others):
+        blocks = [v[k] for k in chunks for v in (own, *others)]
+        return whole_rows(blocks, index, n_chunk)
+
+    scatter(g_q, h1, got[0])
+    out_hidden = order(place_out, out_own, out_peer, out_core, core_swap(out_peer))
+    scatter(g_k, h1, got[1])
+    scatter(g_v, h1, got[2])
+    back_blocks = []
+    for own in back_parts:
+        peer = chip_swap(own)
+        back_blocks += [own, peer, core_swap(own), core_swap(peer)]
+    grad_hidden = order(lambda first, *rest: whole_rows([first, *rest], index, n_chunk), *back_blocks)
+    grad_down, grad_gate, grad_up = [
+        v[0].astype(F32) + dp_swap(v[1]).astype(F32)
+        for v in (after(v, *g_in) for v in (s_down, s_gate, s_up))
+    ]
+    gain_a_part, gain_f_part, loss_part = sum(gain_a_parts), sum(gain_f_parts), sum(loss_parts)
+    small = jnp.concatenate(
+        [own_first(gain_a_part, dp_index), own_first(gain_f_part, dp_index), jnp.full((128,), loss_part)]
+    )
+    small = all_sum(small.reshape(-1, 128)).reshape(-1)
+    at = (dp_index * n_chunk + ctx_index) * share
+    shape = hidden_in.shape
+    return (
+        out_hidden.reshape(shape),
+        small[2 * width] / (count * width),
+        grad_hidden.reshape(shape),
+        *scattered[1:],
+        scattered[0].T,
+        grad_gate,
+        grad_up,
+        grad_down.T,
+        lax.dynamic_slice_in_dim(small, at, share),
+        lax.dynamic_slice_in_dim(small, width + at, share),
+    )
 
 
 def shifted(value, axis, steps):
@@ -24,22 +685,6 @@
 
 def silu(v):
     return v * jax.nn.sigmoid(v)
-
-
-def plain_dot(left, right):
-    return jnp.dot(left, right, preferred_element_type=jnp.float32)
-
-
-def left_dot(left, right):
-    return lax.dot_general(
-        left, right, (((0,), (0,)), ((), ())), preferred_element_type=jnp.float32
-    )
-
-
-def right_dot(left, right):
-    return lax.dot_general(
-        left, right, (((1,), (1,)), ((), ())), preferred_element_type=jnp.float32
-    )
 
 
 def gain_norm(values, gain):
@@ -310,6 +955,8 @@
         P(("dp", "ctx")),
         P(("dp", "ctx")),
     )
+    slots = 8 // mesh.shape["dp"]
+    whole_slots = mesh.shape["ctx"] == slots and mesh.shape["mp"] == 4
     return jax.shard_map(
-        on_device, mesh=mesh, in_specs=in_specs, out_specs=out_specs, check_vma=False
+        slot_device if whole_slots else on_device, mesh=mesh, in_specs=in_specs, out_specs=out_specs, check_vma=False
     )

time: 3640 us -> 1220 us (0.34)
  waiting for transfers between devices: 2630 us -> 480 us
  matrix products: 460 us -> 286 us
  blocking collectives: 140 us -> 0 us
  other arithmetic: 209 us -> 118 us
  Pallas kernels: 0 us -> 83.1 us
  starting transfers between devices: 54.3 us -> 107 us
    psum x4 -> x0, waiting for transfers between devices: 1010 us -> none  [the longest x1 288 us: on_device(): lax.psum(right_dot(grad_gate, full_gate) + right_dot(grad_upper, full_up)...]
    reduce_scatter x7 -> x3, waiting for transfers between devices: 863 us -> 0.01 us  [both_scatter(): return lax.psum_scatter(halves, 'ctx', scatter_dimension=1, tiled=True)]
    all_gather x7 -> x8, waiting for transfers between devices: 356 us -> 6.89 us  [the longest x6 6.89 us: slot_device(): parts.append(lax.all_gather(shard, 'ctx', axis=0, tiled=True))]
    dot_general x54 -> x50, matrix products: 460 us -> 286 us  [dot_t(): return lax.dot_general(a, b, (dims, ((), ())), preferred_element_type=F32)]
    all_gather x2 -> x0, blocking collectives: 100 us -> none  [the longest x1 77.9 us: fetch_feed(): lax.all_gather(feed_gain, ('dp', 'ctx'), axis=0, tiled=True)]
    reduce_sum x9 -> x11, other arithmetic: 101 us -> 13.1 us  [the longest x2 5.06 us: step(): return (grad.astype(BF), grad, result.astype(BF), jnp.sum(error * error))]
    pallas_call x0 -> x6, Pallas kernels: none -> 83.1 us  [the longest x4 67.4 us: attend_call(): pl.pallas_call(lambda *refs: kernel(pair, per, back, *refs), grid_spec=pl...]
    ppermute x16 -> x94, waiting for transfers between devices: 392 us -> 473 us  [the longest x24 234 us: chip_swap(): return lax.ppermute(v, 'mp', [(i, i ^ 2) for i in range(4)])]
  transfers between devices with their start and end apart: 34 -> 105, of which waited for: 21 -> 43; matrix products, arithmetic and copies ran while one was open for 14% -> 35% of each run, Pallas kernels for 0% -> 7%
where the time goes in v1:
time: 1220 us
  waiting for transfers between devices  480 us (39%)
  matrix products  286 us (23%)
  local copies, waits for them, and re-layouts  120 us (10%)
  other arithmetic  118 us (10%)
  starting transfers between devices  107 us (9%)
  Pallas kernels  83.1 us (7%)
  between operations  20.4 us (2%)
    dot_general x50, matrix products, dot_t(): return lax.dot_general(a, b, (dims, ((), ())), preferred_element_type=F32)  286 us
    ppermute x24, waiting for transfers between devices, chip_swap(): return lax.ppermute(v, 'mp', [(i, i ^ 2) for i in range(4)])  234 us
    ppermute x15, waiting for transfers between devices, dp_swap(): return lax.ppermute(v, 'dp', [(i, i ^ 1) for i in range(2)])  159 us
    ppermute x24, waiting for transfers between devices, ctx_turn(): return lax.ppermute(v, 'ctx', [(i, (i + steps) % n) for i in range(n)])  73.3 us
    pallas_call x4, Pallas kernels, attend_call(): pl.pallas_call(lambda *refs: kernel(pair, per, back, *refs), grid_spec=pl...  67.4 us
    ppermute x24, starting transfers between devices, ctx_turn(): return lax.ppermute(v, 'ctx', [(i, (i + steps) % n) for i in range(n)])  49.7 us
    unnamed x348, local copies, waits for them, and re-layouts  48.1 us
    ppermute x24, starting transfers between devices, chip_swap(): return lax.ppermute(v, 'mp', [(i, i ^ 2) for i in range(4)])  32.3 us
  transfers between devices with their start and end apart: 105, of which 43 were waited for; matrix products, arithmetic and copies ran while one was open for 35% of the time, Pallas kernels for 7%

profile of v1, /device:TPU:0, one launch (start us, length us, event | category | flops | bytes accessed | tf_op | source)
XLA Modules:
  0.0 1215.3 jit_solution(10154369272657855290)
XLA Ops:
  21.7 18.3 %collective-permute-done = bf16[128,2048]{1,0:T(8,128)(2,1)S(1)} collective-permute-done((bf16[128,2048]{1,0:T(8,128)(2,1)S(1)}, bf16[128,2048]{1,0:T(8,128)(2,1)S(1)}, u32[]{:S(2)}, u32[]{:S(2)}) %collective-permute-start) | collective-permute-done | bytes 524320 | tf_op jit(solution)/shard_map/ppermute | solution.py:172
  40.0 32.2 %collective-permute-done.1 = bf16[128,2048]{1,0:T(8,128)(2,1)S(1)} collective-permute-done((bf16[128,2048]{1,0:T(8,128)(2,1)S(1)}, bf16[128,2048]{1,0:T(8,128)(2,1)S(1)}, u32[]{:S(2)}, u32[]{:S(2)}) %collective-permute-start.1) | collective-permute-done | bytes 524320 | tf_op jit(solution)/shard_map/ppermute | solution.py:172
  76.0 11.3 collective-permute-done.3
  184.9 12.0 collective-permute-done.13
  240.3 16.4 %attend1.1 = (bf16[1024,512]{1,0:T(8,128)(2,1)}, f32[4,2,512]{2,1,0:T(2,128)}) custom-call(s32[1]{0:T(128)} %bitcast.31.refs_0_, s32[512,1]{1,0:T(8,128)} %fusion.99.refs_1_, s32[1,512]{1,0:T(1,128)} %fusion.109.refs_2_, bf16[1024,512]{1,0:T(8,128)(2,1)} %convolution_convert_fusion.4.refs_3_, bf16[1024,512]{1,0:T(8,128)(2,1)} %convolution_convert_fusion.6.refs_4_.refs_6_, ...), custom_call_target="tpu_custom_call" | custom-call | flops 19327352832 | bytes 7340032 | tf_op jit(solution)/shard_map/attend1/pallas_call | solution.py:135
  296.4 44.8 %collective-permute-done.20 = bf16[1024,1376]{0,1:T(8,128)(2,1)} collective-permute-done((bf16[1024,1376]{0,1:T(8,128)(2,1)}, bf16[1024,1376]{0,1:T(8,128)(2,1)}, u32[]{:S(2)}, u32[]{:S(2)}) %collective-permute-start.20) | collective-permute-done | bytes 2818080 | tf_op jit(solution)/shard_map/ppermute | solution.py:167
  350.7 50.4 %collective-permute-done.23 = bf16[1024,1376]{0,1:T(8,128)(2,1)S(1)} collective-permute-done((bf16[1024,1376]{0,1:T(8,128)(2,1)}, bf16[1024,1376]{0,1:T(8,128)(2,1)S(1)}, u32[]{:S(2)}, u32[]{:S(2)}) %collective-permute-start.23) | collective-permute-done | bytes 2818080 | tf_op jit(solution)/shard_map/ppermute | solution.py:167
  404.1 11.9 collective-permute-start.25
  448.5 12.1 multiply_convert_fusion.5
  469.8 12.2 %multiply_convert_fusion.4 = (bf16[1024,1376]{0,1:T(8,128)(2,1)S(1)}, f32[1024,1376]{0,1:T(8,128)}) fusion(f32[1024,1376]{0,1:T(8,128)S(1)} %fusion.124, bf16[1024,2048]{1,0:T(8,128)(2,1)S(1)} %bitcast.381, bf16[2048,1376]{0,1:T(8,128)(2,1)} %constant_dynamic-update-slice_fusion.8), kind=kOutput, calls=%fused_computation.23 | convolution fusion | flops 5779816448 | bytes 23920640 | tf_op jit(solution)/shard_map/dot_general | solution.py:18
  518.7 19.2 %collective-permute-done.30 = bf16[2,128,2048]{2,1,0:T(8,128)(2,1)S(1)} collective-permute-done((bf16[2,128,2048]{2,1,0:T(8,128)(2,1)S(1)}, bf16[2,128,2048]{2,1,0:T(8,128)(2,1)S(1)}, u32[]{:S(2)}, u32[]{:S(2)}) %collective-permute-start.30) | collective-permute-done | bytes 1048608 | tf_op jit(solution)/shard_map/ppermute | solution.py:163
  542.2 18.2 %collective-permute-done.32 = bf16[2,128,2048]{2,1,0:T(8,128)(2,1)S(1)} collective-permute-done((bf16[2,128,2048]{2,1,0:T(8,128)(2,1)S(1)}, bf16[2,128,2048]{2,1,0:T(8,128)(2,1)S(1)}, u32[]{:S(2)}, u32[]{:S(2)}) %collective-permute-start.32) | collective-permute-done | bytes 1048608 | tf_op jit(solution)/shard_map/ppermute | solution.py:163
  563.1 18.8 %collective-permute-done.34 = bf16[2,128,2048]{2,1,0:T(8,128)(2,1)S(1)} collective-permute-done((bf16[2,128,2048]{2,1,0:T(8,128)(2,1)S(1)}, bf16[2,128,2048]{2,1,0:T(8,128)(2,1)S(1)}, u32[]{:S(2)}, u32[]{:S(2)}) %collective-permute-start.34) | collective-permute-done | bytes 1048608 | tf_op jit(solution)/shard_map/ppermute | solution.py:163
  641.1 11.7 multiply_convert_fusion.1
  665.9 11.4 fusion.133
  732.8 20.5 %collective-permute-done.40 = bf16[2,128,2048]{2,1,0:T(8,128)(2,1)S(1)} collective-permute-done((bf16[2,128,2048]{2,1,0:T(8,128)(2,1)S(1)}, bf16[2,128,2048]{2,1,0:T(8,128)(2,1)S(1)}, u32[]{:S(2)}, u32[]{:S(2)}) %collective-permute-start.40) | collective-permute-done | bytes 1048608 | tf_op jit(solution)/shard_map/ppermute | solution.py:163
  757.7 18.0 %collective-permute-done.39 = bf16[2,128,2048]{2,1,0:T(8,128)(2,1)S(1)} collective-permute-done((bf16[2,128,2048]{2,1,0:T(8,128)(2,1)S(1)}, bf16[2,128,2048]{2,1,0:T(8,128)(2,1)S(1)}, u32[]{:S(2)}, u32[]{:S(2)}) %collective-permute-start.39) | collective-permute-done | bytes 1048608 | tf_op jit(solution)/shard_map/ppermute | solution.py:163
  778.6 18.7 %collective-permute-done.42 = bf16[2,128,2048]{2,1,0:T(8,128)(2,1)S(1)} collective-permute-done((bf16[2,128,2048]{2,1,0:T(8,128)(2,1)S(1)}, bf16[2,128,2048]{2,1,0:T(8,128)(2,1)S(1)}, u32[]{:S(2)}, u32[]{:S(2)}) %collective-permute-start.42) | collective-permute-done | bytes 1048608 | tf_op jit(solution)/shard_map/ppermute | solution.py:163
  808.6 14.7 %attend_back0.1 = (bf16[1024,512]{1,0:T(8,128)(2,1)}, f32[1024,512]{1,0:T(8,128)}, f32[1024,512]{1,0:T(8,128)}) custom-call(s32[1]{0:T(128)} %bitcast.31.refs_0_, s32[512,1]{1,0:T(8,128)} %fusion.99.refs_1_, s32[1,512]{1,0:T(1,128)} %fusion.109.refs_2_, bf16[1024,512]{1,0:T(8,128)(2,1)} %convolution_convert_fusion.7.refs_3_, ...), custom_call_target="tpu_custom_call" | custom-call | flops 24159191040 | bytes 7340032 | tf_op jit(solution)/shard_map/attend_back0/pallas_call | solution.py:135
  852.1 25.7 %attend_back1.1 = (bf16[1024,512]{1,0:T(8,128)(2,1)}, bf16[1024,512]{1,0:T(8,128)(2,1)}, bf16[1024,512]{1,0:T(8,128)(2,1)}, bf16[1024,512]{1,0:T(8,128)(2,1)}, bf16[1024,512]{1,0:T(8,128)(2,1)}) custom-call(s32[1]{0:T(128)} %bitcast.31.refs_0_, s32[512,1]{1,0:T(8,128)} %fusion.99.refs_1_, s32[1,512]{1,0:T(1,128)} %fusion.109.refs_2_, ...), custom_call_target="tpu_custom_call" | custom-call | flops 48318382080 | bytes 13631488 | tf_op jit(solution)/shard_map/attend_back1/pallas_call | solution.py:135
  953.7 26.0 %collective-permute-done.54 = bf16[4,128,2048]{2,1,0:T(8,128)(2,1)} collective-permute-done((bf16[4,128,2048]{2,1,0:T(8,128)(2,1)S(1)}, bf16[4,128,2048]{2,1,0:T(8,128)(2,1)}, u32[]{:S(2)}, u32[]{:S(2)}) %collective-permute-start.54) | collective-permute-done | bytes 2097184 | tf_op jit(solution)/shard_map/ppermute | solution.py:163
  983.0 19.1 %collective-permute-done.51 = bf16[2,128,2048]{2,1,0:T(8,128)(2,1)S(1)} collective-permute-done((bf16[2,128,2048]{2,1,0:T(8,128)(2,1)}, bf16[2,128,2048]{2,1,0:T(8,128)(2,1)S(1)}, u32[]{:S(2)}, u32[]{:S(2)}) %collective-permute-start.51) | collective-permute-done | bytes 1048608 | tf_op jit(solution)/shard_map/ppermute | solution.py:163
  1004.6 19.1 %collective-permute-done.50 = bf16[2,128,2048]{2,1,0:T(8,128)(2,1)S(1)} collective-permute-done((bf16[2,128,2048]{2,1,0:T(8,128)(2,1)S(1)}, bf16[2,128,2048]{2,1,0:T(8,128)(2,1)S(1)}, u32[]{:S(2)}, u32[]{:S(2)}) %collective-permute-start.50) | collective-permute-done | bytes 1048608 | tf_op jit(solution)/shard_map/ppermute | solution.py:163
  1092.3 23.8 %collective-permute-done.92 = bf16[256,1376]{0,1:T(8,128)(2,1)S(1)} collective-permute-done((bf16[256,1376]{0,1:T(8,128)(2,1)}, bf16[256,1376]{0,1:T(8,128)(2,1)S(1)}, u32[]{:S(2)}, u32[]{:S(2)}) %collective-permute-start.92) | collective-permute-done | bytes 704544 | tf_op jit(solution)/shard_map/ppermute | solution.py:167
  (781 shorter events, 708.4 us)
Async XLA Ops:
  7.2 68.8 %all-gather.9.cloned.1.call-start = ((), (), s32[]{:S(2)}) async-start(), calls=%async_computation.3 | async-start | bytes 1392640 | tf_op jit(solution)/shard_map/all_gather | solution.py:383
  10.3 118.7 %all-gather.11.cloned.1.call-start = ((), (), s32[]{:S(2)}) async-start(), calls=%async_computation.4 | async-start | bytes 1310720 | tf_op jit(solution)/shard_map/all_gather | solution.py:383
  72.3 67.5 %all-gather.15.cloned.1.call-start = ((), (), s32[]{:S(2)}) async-start(), calls=%async_computation.6 | async-start | bytes 1310720 | tf_op jit(solution)/shard_map/all_gather | solution.py:383
  76.0 105.8 %all-gather.13.cloned.1.call-start = ((), (), s32[]{:S(2)}) async-start(), calls=%async_computation.5 | async-start | bytes 1310720 | tf_op jit(solution)/shard_map/all_gather | solution.py:383
  129.6 110.4 %all-gather.17.cloned.1.call-start = ((), (), s32[]{:S(2)}) async-start(), calls=%async_computation.7 | async-start | bytes 3522560 | tf_op jit(solution)/shard_map/all_gather | solution.py:383
  139.8 146.6 %all-gather.19.cloned.1.call-start = ((), (), s32[]{:S(2)}) async-start(), calls=%async_computation.8 | async-start | bytes 3522560 | tf_op jit(solution)/shard_map/all_gather | solution.py:383
  183.4 242.9 %all-gather.21.cloned.1.call-start = ((), (), s32[]{:S(2)}) async-start(), calls=%async_computation.9 | async-start | bytes 3522560 | tf_op jit(solution)/shard_map/all_gather | solution.py:386
  240.0 189.9 %all-gather.23.cloned.1.call-start = ((), (), s32[]{:S(2)}) async-start(), calls=%async_computation.10 | async-start | bytes 3522560 | tf_op jit(solution)/shard_map/all_gather | solution.py:386
  264.5 76.7 %collective-permute-start.20 = (bf16[1024,1376]{0,1:T(8,128)(2,1)}, bf16[1024,1376]{0,1:T(8,128)(2,1)}, u32[]{:S(2)}, u32[]{:S(2)}) collective-permute-start(bf16[1024,1376]{0,1:T(8,128)(2,1)} %all-gather.17.cloned.1.call-done), channel_id=1, source_target_pairs={{0,16},{16,0},{1,17},{17,1},{2,18},{18,2},{3,19},{19,3},{4,20},{20... | collective-permute-start | bytes 8454152 | tf_op jit(solution)/shard_map/ppermute | solution.py:167
  280.8 609.7 %reduce-scatter.4.cloned.1.call-start = ((), (), s32[]{:S(2)}) async-start(), calls=%async_computation.11 | async-start | bytes 7045120 | tf_op jit(solution)/shard_map/reduce_scatter | solution.py:248
  286.5 114.6 %collective-permute-start.23 = (bf16[1024,1376]{0,1:T(8,128)(2,1)}, bf16[1024,1376]{0,1:T(8,128)(2,1)S(1)}, u32[]{:S(2)}, u32[]{:S(2)}) collective-permute-start(bf16[1024,1376]{0,1:T(8,128)(2,1)} %all-gather.19.cloned.1.call-done), channel_id=1, source_target_pairs={{0,16},{16,0},{1,17},{17,1},{2,18},{18,2},{3,19},{19,3},{4,20},{20... | collective-permute-start | bytes 8454152 | tf_op jit(solution)/shard_map/ppermute | solution.py:167
  350.7 83.0 %collective-permute-start.21 = (bf16[2,256,2048]{2,1,0:T(8,128)(2,1)}, bf16[2,256,2048]{2,1,0:T(8,128)(2,1)}, u32[]{:S(2)}, u32[]{:S(2)}) collective-permute-start(bf16[2,256,2048]{2,1,0:T(8,128)(2,1)} %pad_maximum_fusion.12), channel_id=1, source_target_pairs={{0,1},{1,0},{2,3},{3,2},{4,5},{5,4},{6,7},{7,6},{8,9},{9,8},{10,11... | collective-permute-start | bytes 6291464 | tf_op jit(solution)/shard_map/ppermute | solution.py:159
  665.8 360.4 %reduce-scatter.8.cloned.1.call-start = ((), (), s32[]{:S(2)}) async-start(), calls=%async_computation.13 | async-start | bytes 7045120 | tf_op jit(solution)/shard_map/reduce_scatter | solution.py:248
  727.1 301.6 %reduce-scatter.6.cloned.1.call-start = ((), (), s32[]{:S(2)}) async-start(), calls=%async_computation.12 | async-start | bytes 7045120 | tf_op jit(solution)/shard_map/reduce_scatter | solution.py:248
  837.4 90.3 %collective-permute-start.45 = (bf16[128,2048]{1,0:T(8,128)(2,1)}, bf16[128,2048]{1,0:T(8,128)(2,1)}, u32[]{:S(2)}, u32[]{:S(2)}) collective-permute-start(bf16[128,2048]{1,0:T(8,128)(2,1)} %get-tuple-element.273), channel_id=1, source_target_pairs={{0,4},{4,8},{8,12},{12,0},{1,5},{5,9},{9,13},{13,1},{2,6},{6,10},{... | collective-permute-start | bytes 1572872 | tf_op jit(solution)/shard_map/ppermute | solution.py:172
  839.2 90.2 %collective-permute-start.46 = (bf16[128,2048]{1,0:T(8,128)(2,1)}, bf16[128,2048]{1,0:T(8,128)(2,1)}, u32[]{:S(2)}, u32[]{:S(2)}) collective-permute-start(bf16[128,2048]{1,0:T(8,128)(2,1)} %get-tuple-element.272), channel_id=1, source_target_pairs={{0,8},{4,12},{8,0},{12,4},{1,9},{5,13},{9,1},{13,5},{2,10},{6,14},... | collective-permute-start | bytes 1572872 | tf_op jit(solution)/shard_map/ppermute | solution.py:172
  841.6 87.9 %collective-permute-start.47 = (bf16[128,2048]{1,0:T(8,128)(2,1)S(1)}, bf16[128,2048]{1,0:T(8,128)(2,1)}, u32[]{:S(2)}, u32[]{:S(2)}) collective-permute-start(bf16[128,2048]{1,0:T(8,128)(2,1)S(1)} %get-tuple-element.271), channel_id=1, source_target_pairs={{0,12},{4,0},{8,4},{12,8},{1,13},{5,1},{9,5},{13,9},{2,14},{6,2},{... | collective-permute-start | bytes 1572872 | tf_op jit(solution)/shard_map/ppermute | solution.py:172
  927.7 106.0 %collective-permute-start.52 = (bf16[1024,512]{1,0:T(8,128)(2,1)}, bf16[1024,512]{1,0:T(8,128)(2,1)}, u32[]{:S(2)}, u32[]{:S(2)}) collective-permute-start(bf16[1024,512]{1,0:T(8,128)(2,1)} %add_convert_fusion.10), channel_id=1, source_target_pairs={{0,16},{16,0},{1,17},{17,1},{2,18},{18,2},{3,19},{19,3},{4,20},{20... | collective-permute-start | bytes 3145736 | tf_op jit(solution)/shard_map/ppermute | solution.py:167
  938.2 63.9 %collective-permute-start.51 = (bf16[2,128,2048]{2,1,0:T(8,128)(2,1)}, bf16[2,128,2048]{2,1,0:T(8,128)(2,1)S(1)}, u32[]{:S(2)}, u32[]{:S(2)}) collective-permute-start(bf16[2,128,2048]{2,1,0:T(8,128)(2,1)} %slice.588), channel_id=1, source_target_pairs={{0,2},{1,3},{2,0},{3,1},{4,6},{5,7},{6,4},{7,5},{8,10},{9,11},{10,... | collective-permute-start | bytes 3145736 | tf_op jit(solution)/shard_map/ppermute | solution.py:163
  944.8 78.9 %collective-permute-start.50 = (bf16[2,128,2048]{2,1,0:T(8,128)(2,1)S(1)}, bf16[2,128,2048]{2,1,0:T(8,128)(2,1)S(1)}, u32[]{:S(2)}, u32[]{:S(2)}) collective-permute-start(bf16[2,128,2048]{2,1,0:T(8,128)(2,1)S(1)} %slice.587), channel_id=1, source_target_pairs={{0,2},{1,3},{2,0},{3,1},{4,6},{5,7},{6,4},{7,5},{8,10},{9,11},{10,... | collective-permute-start | bytes 3145736 | tf_op jit(solution)/shard_map/ppermute | solution.py:163
  952.9 93.1 %collective-permute-start.53 = (bf16[1024,512]{1,0:T(8,128)(2,1)}, bf16[1024,512]{1,0:T(8,128)(2,1)}, u32[]{:S(2)}, u32[]{:S(2)}) collective-permute-start(bf16[1024,512]{1,0:T(8,128)(2,1)} %add_convert_fusion.9), channel_id=1, source_target_pairs={{0,16},{16,0},{1,17},{17,1},{2,18},{18,2},{3,19},{19,3},{4,20},{20... | collective-permute-start | bytes 3145736 | tf_op jit(solution)/shard_map/ppermute | solution.py:167
  979.7 150.7 %collective-permute-start.62 = (bf16[1024,512]{1,0:T(8,128)(2,1)}, bf16[1024,512]{1,0:T(8,128)(2,1)}, u32[]{:S(2)}, u32[]{:S(2)}) collective-permute-start(bf16[1024,512]{1,0:T(8,128)(2,1)} %add_convert_fusion.8), channel_id=1, source_target_pairs={{0,16},{16,0},{1,17},{17,1},{2,18},{18,2},{3,19},{19,3},{4,20},{20... | collective-permute-start | bytes 3145736 | tf_op jit(solution)/shard_map/ppermute | solution.py:167
  1002.1 115.3 %collective-permute-start.56 = (bf16[4,128,2048]{2,1,0:T(8,128)(2,1)}, bf16[4,128,2048]{2,1,0:T(8,128)(2,1)}, u32[]{:S(2)}, u32[]{:S(2)}) collective-permute-start(bf16[4,128,2048]{2,1,0:T(8,128)(2,1)} %collective-permute-done.54), channel_id=1, source_target_pairs={{0,1},{1,0},{2,3},{3,2},{4,5},{5,4},{6,7},{7,6},{8,9},{9,8},{10,11... | collective-permute-start | bytes 6291464 | tf_op jit(solution)/shard_map/ppermute | solution.py:159
  1028.2 61.3 %collective-permute-start.93 = (bf16[256,1376]{0,1:T(8,128)(2,1)}, bf16[256,1376]{0,1:T(8,128)(2,1)}, u32[]{:S(2)}, u32[]{:S(2)}) collective-permute-start(bf16[256,1376]{0,1:T(8,128)(2,1)} %slice_bitcast_fusion), channel_id=1, source_target_pairs={{0,16},{16,0},{1,17},{17,1},{2,18},{18,2},{3,19},{19,3},{4,20},{20... | collective-permute-start | bytes 2113544 | tf_op jit(solution)/shard_map/ppermute | solution.py:167
  (248 other events, 4279.0 us)
Sparse Core Ops, SparseCore 0:
  10.4 59.9 all-gather.8
  72.4 38.2 all-gather.10
  112.3 27.4 all-gather.14
  141.2 29.6 all-gather.12
  172.3 56.3 all-gather.16
  230.2 56.2 all-gather.18
  288.0 56.2 all-gather.20
  345.9 56.2 all-gather.22
  665.9 101.3 reduce-scatter.3
  769.4 134.3 reduce-scatter.7
  906.1 101.7 reduce-scatter.5

commit v2 on v1

--- a/solution.py
+++ b/solution.py
@@ -147,9 +147,9 @@
         out_shape=shapes,
         compiler_params=pltpu.CompilerParams(vmem_limit_bytes=56 << 20),
         cost_estimate=pl.CostEstimate(
-            flops=6 * n_dots * blocks * rows * rows * HEAD_DIM * heads,
-            bytes_accessed=2 * wide * cols * (len(ins) + len(shapes)),
-            transcendentals=blocks * rows * rows * heads,
+            flops=n_dots * blocks * rows * rows * HEAD_DIM * heads,
+            bytes_accessed=1 << 16 if lses else 2 * wide * cols * (len(ins) + len(shapes)),
+            transcendentals=0 if lses else blocks * rows * rows * heads,
         ),
         name=f"{name}{pair}",
     )(length, kcol, qrow, *((*ins[:2], *lses, *ins[2:]) if lses else ins))
@@ -244,18 +244,10 @@
 
 
 def both_scatter(grad):
-    halves = grad.reshape(2, -1, grad.shape[1])
-    return lax.psum_scatter(halves, "ctx", scatter_dimension=1, tiled=True)
-
-
-def ring_scatter(grad, z):
-    n = lax.axis_size("ctx")
-    blocks = grad.reshape(n, -1, grad.shape[1])
-    travel = pick(blocks, (z + n - 1) % n)
-    for k in range(2, n + 1):
-        total = pick(blocks, (z + n - k) % n).astype(F32) + ctx_turn(travel, 1).astype(F32)
-        travel = total.astype(BF)
-    return total
+    half = grad.shape[0] // 2
+    swapped = jnp.concatenate([grad[half:], grad[:half]], axis=0)
+    grad = jnp.where(lax.axis_index("dp") == 0, grad, swapped)
+    return lax.psum_scatter(grad, ("dp", "ctx"), scatter_dimension=0, tiled=True)
 
 
 def to_slots(v, z):
@@ -436,7 +428,7 @@
                 jax.ShapeDtypeStruct((heads, per, group), F32),
             ]
             return attend_call(
-                attend_kernel, "attend", p, per, back, kcol, qrow, length, ins, [], shapes, 4
+                attend_kernel, "attend", p, per, back, kcol, qrow, length, ins, [], shapes, 24
             )
 
         a, l = order(step, queries[p])
@@ -466,13 +458,13 @@
         sent[p], kept[p] = order(lambda a: split_part(right_dot(a, w_out), per), attended[p])
     pass_core(0)
     pass_core(1)
+    order.wait(fetched[4][1])
     low = [enter_feed(0)]
-    order.wait(part_up, fetched[4][1])
+    order.wait(part_up)
     low.append(enter_feed(1))
-    low[0] = gather_half(low[0])
+    low = [gather_half(v) for v in low]
     order.wait(fetched[5][1])
-    low[1] = gather_half(low[1])
-    h2 += [gather_rest(v) for v in low]
+    h2.append(gather_rest(low[0]))
 
     gate, up, hidden, results, g_result, g_branch, loss_parts = [], [], [], [], [], [], []
 
@@ -495,20 +487,14 @@
         loss_parts.append(loss)
         return low
 
-    for p in pairs:
+    def feed(p):
         h, g, u = order(unit, h2[p])
         hidden.append(h)
         gate.append(g)
         up.append(u)
-        if p == 0:
-            order.wait(*teacher_parts)
-    for p in pairs:
+
+    def project_down(p):
         sent[p], kept[p] = order(lambda h: split_part(right_dot(h, w_down), per), hidden[p])
-    pass_core(0)
-    pass_core(1)
-    low = [finish(0), finish(1)]
-    low[0] = gather_half(low[0])
-    g_branch.append(gather_rest(low[0]))
 
     g_gate, g_up, g_mid, g_att, gain_f_parts = [], [], [], [], []
 
@@ -547,30 +533,11 @@
     def scatter(rights, lefts, got):
         part = order(own_part_grad, rights[0], lefts[0])
         own = order(own_rest, rights[1], lefts[1], part, got)
-        scattered.append(ring_scatter(own, ctx_index))
+        scattered.append(lax.psum_scatter(own, "ctx", scatter_dimension=0, tiled=True))
 
     def send(rights, lefts):
         part = order(their_part, rights[0], lefts[0])
         return dp_swap(order(their_rest, rights[1], lefts[1], part))
-
-    part = order(whole_part, hidden[0], g_branch[0])
-    leave_unit(0)
-    low[1] = gather_half(low[1])
-    gate_part = order(whole_part, g_gate[0], h2[0])
-    g_branch.append(gather_rest(low[1]))
-    d_down = order(whole_rest, hidden[1], g_branch[1], part)
-    s_down = both_scatter(d_down)
-    leave_unit(1)
-    s_gate = both_scatter(order(whole_rest, g_gate[1], h2[1], gate_part))
-    up_part = order(whole_part, g_up[0], h2[0])
-    s_up = both_scatter(order(whole_rest, g_up[1], h2[1], up_part))
-    project_unit(0)
-    pass_core(0)
-    project_unit(1)
-    pass_core(1)
-    low = [enter_attention(0), enter_attention(1)]
-    low[0] = gather_half(low[0])
-    g_att.append(gather_rest(low[0]))
 
     g_q, g_k, g_v = [None] * len(pairs), [None] * len(pairs), [None] * len(pairs)
     g_in, gain_a_parts = [], []
@@ -586,7 +553,7 @@
             shapes = [jax.ShapeDtypeStruct(shape, kind) for kind in [BF] + kinds * 2]
             return attend_call(
                 attend_back_kernel, "attend_back", p, per, back, kcol, qrow, length,
-                [*ins, *g_k[first:p], *g_v[first:p]], [lse[p]], shapes, 10,
+                [*ins, *g_k[first:p], *g_v[first:p]], [lse[p]], shapes, 0,
             )
 
         out = order(step, g_att[p])
@@ -612,26 +579,57 @@
         g_in.append(low)
         gain_a_parts.append(g_gain)
 
+    feed(0)
+    order.wait(*teacher_parts)
+    project_down(0)
+    h2.append(gather_rest(low[1]))
+    pass_core(0)
+    feed(1)
+    first = finish(0)
+    project_down(1)
+    pass_core(1)
+    g_branch.append(gather_rest(gather_half(first)))
+    leave_unit(0)
+    part = order(whole_part, hidden[0], g_branch[0])
+    second = finish(1)
+    out_parts = to_slots(own_first(jnp.concatenate(results, axis=0), dp_index), ctx_index)
+    project_unit(0)
+    pass_core(0)
+    order.wait(*out_parts)
+    g_branch.append(gather_rest(gather_half(second)))
+    leave_unit(1)
+    s_down = both_scatter(order(whole_rest, hidden[1], g_branch[1], part))
+    first = enter_attention(0)
+    project_unit(1)
+    pass_core(1)
+    part = order(whole_part, g_gate[0], h2[0])
+    s_gate = both_scatter(order(whole_rest, g_gate[1], h2[1], part))
+    g_att.append(gather_rest(gather_half(first)))
     attention_back(0)
-    low[1] = gather_half(low[1])
-    g_att.append(gather_rest(low[1]))
-    results = [after(v, low[1]) for v in results]
-    out_parts = to_slots(own_first(jnp.concatenate(results, axis=0), dp_index), ctx_index)
+    order.wait(s_down)
+    second = enter_attention(1)
+    g_att.append(gather_rest(gather_half(second)))
+    part = order(whole_part, g_up[0], h2[0])
+    s_up = both_scatter(order(whole_rest, g_up[1], h2[1], part))
     out_got = send(attended, g_att)
-    attention_back(1)
-    order.wait(s_gate)
-    project_back(0)
-    project_back(1)
     out_own = order(lambda first, *rest: jnp.stack([first, *rest]), *out_parts)
     out_peer, out_core = chip_swap(out_own), core_swap(out_own)
+    attention_back(1)
+    order.wait(out_peer, out_got)
+    project_back(0)
     pass_core(0)
-    got = [send(g_q, h1)]
+    rights = [
+        order(lambda q, k, v: jnp.concatenate([q, k, v], axis=1), g_q[p], g_k[p], g_v[p]) for p in pairs
+    ]
+    qkv_got = send(rights, h1)
+    order.wait(s_gate)
+    project_back(1)
+    leave(0)
     pass_core(1)
-    got += [send(right, h1) for right in (g_k, g_v)]
-    leave(0)
     leave(1)
     back_parts = to_slots(own_first(jnp.concatenate(g_in, axis=0), dp_index), ctx_index)
     scatter(attended, g_att, out_got)
+    part = order(own_part_grad, rights[0], h1[0])
     slots = [(ctx_index - k) % n_chunk for k in chunks]
     index = [(slot, place ^ i) for slot in slots for i in range(4)]
 
@@ -639,32 +637,32 @@
         blocks = [v[k] for k in chunks for v in (own, *others)]
         return whole_rows(blocks, index, n_chunk)
 
-    scatter(g_q, h1, got[0])
+    order.wait(*back_parts, qkv_got)
     out_hidden = order(place_out, out_own, out_peer, out_core, core_swap(out_peer))
-    scatter(g_k, h1, got[1])
-    scatter(g_v, h1, got[2])
+    back_peers = [chip_swap(own) for own in back_parts]
+    order.wait(s_up, *back_peers)
+    own = order(own_rest, rights[1], h1[1], part, qkv_got)
+    s_qkv = lax.psum_scatter(own, "ctx", scatter_dimension=0, tiled=True).astype(F32)
     back_blocks = []
-    for own in back_parts:
-        peer = chip_swap(own)
+    for own, peer in zip(back_parts, back_peers):
         back_blocks += [own, peer, core_swap(own), core_swap(peer)]
     grad_hidden = order(lambda first, *rest: whole_rows([first, *rest], index, n_chunk), *back_blocks)
-    grad_down, grad_gate, grad_up = [
-        v[0].astype(F32) + dp_swap(v[1]).astype(F32)
-        for v in (after(v, *g_in) for v in (s_down, s_gate, s_up))
-    ]
+    grad_down, grad_gate, grad_up = [v.astype(F32) for v in (s_down, s_gate, s_up)]
     gain_a_part, gain_f_part, loss_part = sum(gain_a_parts), sum(gain_f_parts), sum(loss_parts)
     small = jnp.concatenate(
         [own_first(gain_a_part, dp_index), own_first(gain_f_part, dp_index), jnp.full((128,), loss_part)]
     )
-    small = all_sum(small.reshape(-1, 128)).reshape(-1)
+    small = all_sum(after(small, *back_peers).reshape(-1, 128)).reshape(-1)
     at = (dp_index * n_chunk + ctx_index) * share
     shape = hidden_in.shape
     return (
         out_hidden.reshape(shape),
         small[2 * width] / (count * width),
         grad_hidden.reshape(shape),
-        *scattered[1:],
-        scattered[0].T,
+        s_qkv[:, :cols],
+        s_qkv[:, cols : 2 * cols],
+        s_qkv[:, 2 * cols :],
+        scattered[0].astype(F32).T,
         grad_gate,
         grad_up,
         grad_down.T,

time: 1220 us -> 1190 us (0.975)
  local copies, waits for them, and re-layouts: 120 us -> 92.1 us
  starting transfers between devices: 107 us -> 83.8 us
    ppermute x24, waiting for transfers between devices: 234 us -> 136 us  [chip_swap(): return lax.ppermute(v, 'mp', [(i, i ^ 2) for i in range(4)])]
    reduce_scatter x3 -> x5, waiting for transfers between devices: 0.01 us -> 64.9 us  [the longest x3 40 us: both_scatter(): lax.psum_scatter(grad, ('dp', 'ctx'), scatter_dimension=0, tiled=True)]
    ppermute x15 -> x10, waiting for transfers between devices: 159 us -> 114 us  [dp_swap(): return lax.ppermute(v, 'dp', [(i, i ^ 1) for i in range(2)])]
    ppermute x24 -> x12, waiting for transfers between devices: 73.3 us -> 108 us  [ctx_turn(): return lax.ppermute(v, 'ctx', [(i, (i + steps) % n) for i in range(n)])]
    all_gather x6, waiting for transfers between devices: 6.89 us -> 36.1 us  [slot_device(): parts.append(lax.all_gather(shard, 'ctx', axis=0, tiled=True))]
    ppermute x24 -> x12, starting transfers between devices: 49.7 us -> 21.5 us  [ctx_turn(): return lax.ppermute(v, 'ctx', [(i, (i + steps) % n) for i in range(n)])]
    ppermute x2, starting transfers between devices: 1.98 us -> 15.4 us  [all_sum(): v = v + lax.ppermute(v, 'ctx', [(i, i ^ step) for i in range(n)])]
    select_n x0 -> x3, other arithmetic: none -> 12.2 us  [both_scatter(): grad = jnp.where(lax.axis_index('dp') == 0, grad, swapped)]
  transfers between devices with their start and end apart: 105 -> 90, of which waited for: 43 -> 38; matrix products, arithmetic and copies ran while one was open for 35% -> 36% of each run, Pallas kernels for 7% -> 7%
where the time goes in v2:
time: 1190 us; the launch traced here: 1180 us
  waiting for transfers between devices  489 us (41%)
  matrix products  286 us (24%)
  other arithmetic  121 us (10%)
  local copies, waits for them, and re-layouts  92.1 us (8%)
  Pallas kernels  85.4 us (7%)
  starting transfers between devices  83.8 us (7%)
  between operations  20.7 us (2%)
    dot_general x42, matrix products, dot_t(): return lax.dot_general(a, b, (dims, ((), ())), preferred_element_type=F32)  286 us
    ppermute x24, waiting for transfers between devices, chip_swap(): return lax.ppermute(v, 'mp', [(i, i ^ 2) for i in range(4)])  136 us
    ppermute x10, waiting for transfers between devices, dp_swap(): return lax.ppermute(v, 'dp', [(i, i ^ 1) for i in range(2)])  114 us
    ppermute x12, waiting for transfers between devices, ctx_turn(): return lax.ppermute(v, 'ctx', [(i, (i + steps) % n) for i in range(n)])  108 us
    pallas_call x4, Pallas kernels, attend_call(): pl.pallas_call(lambda *refs: kernel(pair, per, back, *refs), grid_spec=pl...  67.2 us
    unnamed x327, local copies, waits for them, and re-layouts  45.1 us
    reduce_scatter x3, waiting for transfers between devices, both_scatter(): lax.psum_scatter(grad, ('dp', 'ctx'), scatter_dimension=0, tiled=True)  40 us
    all_gather x6, waiting for transfers between devices, slot_device(): parts.append(lax.all_gather(shard, 'ctx', axis=0, tiled=True))  36.1 us
  transfers between devices with their start and end apart: 90, of which 38 were waited for; matrix products, arithmetic and copies ran while one was open for 36% of the time, Pallas kernels for 7%

profile of v2, /device:TPU:0, one launch (start us, length us, event | category | flops | bytes accessed | tf_op | source)
XLA Modules:
  0.0 1177.6 jit_solution(5581527092147143492)
XLA Ops:
  21.7 18.3 %collective-permute-done = bf16[128,2048]{1,0:T(8,128)(2,1)S(1)} collective-permute-done((bf16[128,2048]{1,0:T(8,128)(2,1)S(1)}, bf16[128,2048]{1,0:T(8,128)(2,1)S(1)}, u32[]{:S(2)}, u32[]{:S(2)}) %collective-permute-start) | collective-permute-done | bytes 524320 | tf_op jit(solution)/shard_map/ppermute | solution.py:172
  40.0 32.2 %collective-permute-done.1 = bf16[128,2048]{1,0:T(8,128)(2,1)S(1)} collective-permute-done((bf16[128,2048]{1,0:T(8,128)(2,1)S(1)}, bf16[128,2048]{1,0:T(8,128)(2,1)S(1)}, u32[]{:S(2)}, u32[]{:S(2)}) %collective-permute-start.1) | collective-permute-done | bytes 524320 | tf_op jit(solution)/shard_map/ppermute | solution.py:172
  74.7 36.1 %all-gather.11.cloned.1.call-done = bf16[1024,512]{1,0:T(8,128)(2,1)} async-done(((bf16[256,512]{1,0:T(8,128)(2,1)}), bf16[1024,512]{1,0:T(8,128)(2,1)}) %all-gather.11.cloned.1.call-update) | async-done | bytes 1048592 | tf_op jit(solution)/shard_map/all_gather | solution.py:375
  165.2 13.8 %collective-permute-done.11 = bf16[1088,512]{1,0:T(8,128)(2,1)} collective-permute-done((bf16[1088,512]{1,0:T(8,128)(2,1)S(1)}, bf16[1088,512]{1,0:T(8,128)(2,1)}, u32[]{:S(2)}, u32[]{:S(2)}) %collective-permute-start.11) | collective-permute-done | bytes 1114144 | tf_op jit(solution)/shard_map/ppermute | solution.py:167
  207.9 16.0 %collective-permute-done.13 = bf16[1024,512]{1,0:T(8,128)(2,1)S(1)} collective-permute-done((bf16[1024,512]{1,0:T(8,128)(2,1)S(1)}, bf16[1024,512]{1,0:T(8,128)(2,1)S(1)}, u32[]{:S(2)}, u32[]{:S(2)}) %collective-permute-start.13) | collective-permute-done | bytes 1048608 | tf_op jit(solution)/shard_map/ppermute | solution.py:167
  268.7 16.3 %attend1.1 = (bf16[1024,512]{1,0:T(8,128)(2,1)}, f32[4,2,512]{2,1,0:T(2,128)}) custom-call(s32[1]{0:T(128)} %bitcast.31.refs_0_, s32[512,1]{1,0:T(8,128)} %fusion.62.refs_1_, s32[1,512]{1,0:T(1,128)} %fusion.72.refs_2_, bf16[1024,512]{1,0:T(8,128)(2,1)} %convolution_convert_fusion.4.refs_3_, bf16[1024,512]{1,0:T(8,128)(2,1)} %convolution_convert_fusion.6.refs_4_.refs_6_, ...), custom_call_target="tpu_custom_call" | custom-call | flops 19327352832 | bytes 7340032 | tf_op jit(solution)/shard_map/attend1/pallas_call | solution.py:135
  315.6 11.0 collective-permute-done.16
  326.6 28.4 %collective-permute-done.18 = bf16[1024,1376]{0,1:T(8,128)(2,1)} collective-permute-done((bf16[1024,1376]{0,1:T(8,128)(2,1)}, bf16[1024,1376]{0,1:T(8,128)(2,1)}, u32[]{:S(2)}, u32[]{:S(2)}) %collective-permute-start.18) | collective-permute-done | bytes 2818080 | tf_op jit(solution)/shard_map/ppermute | solution.py:167
  361.5 22.5 %collective-permute-done.19 = bf16[2,128,2048]{2,1,0:T(8,128)(2,1)S(1)} collective-permute-done((bf16[2,128,2048]{2,1,0:T(8,128)(2,1)S(1)}, bf16[2,128,2048]{2,1,0:T(8,128)(2,1)S(1)}, u32[]{:S(2)}, u32[]{:S(2)}) %collective-permute-start.19) | collective-permute-done | bytes 1048608 | tf_op jit(solution)/shard_map/ppermute | solution.py:163
  392.1 22.3 %collective-permute-done.23 = bf16[1024,1376]{0,1:T(8,128)(2,1)S(1)} collective-permute-done((bf16[1024,1376]{0,1:T(8,128)(2,1)}, bf16[1024,1376]{0,1:T(8,128)(2,1)S(1)}, u32[]{:S(2)}, u32[]{:S(2)}) %collective-permute-start.23) | collective-permute-done | bytes 2818080 | tf_op jit(solution)/shard_map/ppermute | solution.py:167
  523.4 18.4 %collective-permute-done.33 = bf16[2,128,2048]{2,1,0:T(8,128)(2,1)S(1)} collective-permute-done((bf16[2,128,2048]{2,1,0:T(8,128)(2,1)S(1)}, bf16[2,128,2048]{2,1,0:T(8,128)(2,1)S(1)}, u32[]{:S(2)}, u32[]{:S(2)}) %collective-permute-start.33) | collective-permute-done | bytes 1048608 | tf_op jit(solution)/shard_map/ppermute | solution.py:163
  546.6 14.5 %multiply_convert_fusion.2 = (bf16[1024,1376]{0,1:T(8,128)(2,1)}, bf16[1024,1376]{0,1:T(8,128)(2,1)}) fusion(f32[1024,1376]{0,1:T(8,128)} %copy-done.133, f32[1024,1376]{0,1:T(8,128)} %get-tuple-element.340, bf16[1024,2048]{1,0:T(8,128)(2,1)S(1)} %bitcast.298, bf16[2048,1376]{0,1:T(8,128)(2,1)} %constant_dynamic-update-slice_fusion.10), kind=kOutput, calls=%fused_computation.23 | convolution fusion | flops 5789679616 | bytes 26738688 | tf_op jit(solution)/shard_map/dot_general | solution.py:18
  561.0 11.8 %fusion.92 = f32[1024,2048]{1,0:T(8,128)} fusion(bf16[1024,1376]{0,1:T(8,128)(2,1)} %get-tuple-element.159, bf16[2048,1376]{0,1:T(8,128)(2,1)} %copy-done.78), kind=kOutput, calls=%fused_computation.339 | convolution fusion | flops 5771362304 | bytes 16842752 | tf_op jit(solution)/shard_map/dot_general | solution.py:18
  616.5 21.5 %collective-permute-done.39 = bf16[128,2048]{1,0:T(8,128)(2,1)S(1)} collective-permute-done((bf16[128,2048]{1,0:T(8,128)(2,1)S(1)}, bf16[128,2048]{1,0:T(8,128)(2,1)S(1)}, u32[]{:S(2)}, u32[]{:S(2)}) %collective-permute-start.39) | collective-permute-done | bytes 524320 | tf_op jit(solution)/shard_map/ppermute | solution.py:172
  642.7 12.1 %multiply_convert_fusion = (bf16[1024,1376]{0,1:T(8,128)(2,1)}, bf16[1024,1376]{0,1:T(8,128)(2,1)}) fusion(f32[1024,1376]{0,1:T(8,128)} %fusion.90, f32[1024,1376]{0,1:T(8,128)} %get-tuple-element.342, bf16[1024,2048]{1,0:T(8,128)(2,1)S(1)} %bitcast.296, bf16[2048,1376]{0,1:T(8,128)(2,1)S(1)} %bitcast.312), kind=kOutput, calls=%fused_computation.21 | convolution fusion | flops 5789679616 | bytes 26738688 | tf_op jit(solution)/shard_map/dot_general | solution.py:18
  726.9 14.7 %attend_back0.1 = (bf16[1024,512]{1,0:T(8,128)(2,1)}, f32[1024,512]{1,0:T(8,128)}, f32[1024,512]{1,0:T(8,128)}) custom-call(s32[1]{0:T(128)} %bitcast.31.refs_0_, s32[512,1]{1,0:T(8,128)} %fusion.62.refs_1_, s32[1,512]{1,0:T(1,128)} %fusion.72.refs_2_, bf16[1024,512]{1,0:T(8,128)(2,1)} %convolution_convert_fusion.7.refs_3_, ...), custom_call_target="tpu_custom_call" | custom-call | bytes 65536 | tf_op jit(solution)/shard_map/attend_back0/pallas_call | solution.py:135
  744.5 40.0 %reduce-scatter.6.cloned.1.call-done = bf16[256,1376]{0,1:T(8,128)(2,1)} async-done(((bf16[2048,1376]{0,1:T(8,128)(2,1)}), bf16[256,1376]{0,1:T(8,128)(2,1)}) %reduce-scatter.6.cloned.1.call-update) | async-done | bytes 704528 | tf_op jit(solution)/shard_map/reduce_scatter | solution.py:250
  793.1 23.3 %collective-permute-done.46 = bf16[2,128,2048]{2,1,0:T(8,128)(2,1)S(1)} collective-permute-done((bf16[2,128,2048]{2,1,0:T(8,128)(2,1)S(1)}, bf16[2,128,2048]{2,1,0:T(8,128)(2,1)S(1)}, u32[]{:S(2)}, u32[]{:S(2)}) %collective-permute-start.46) | collective-permute-done | bytes 1048608 | tf_op jit(solution)/shard_map/ppermute | solution.py:163
  860.6 25.7 %attend_back1.1 = (bf16[1024,512]{1,0:T(8,128)(2,1)}, bf16[1024,512]{1,0:T(8,128)(2,1)}, bf16[1024,512]{1,0:T(8,128)(2,1)}, bf16[1024,512]{1,0:T(8,128)(2,1)}, bf16[1024,512]{1,0:T(8,128)(2,1)}) custom-call(s32[1]{0:T(128)} %bitcast.31.refs_0_, s32[512,1]{1,0:T(8,128)} %fusion.62.refs_1_, s32[1,512]{1,0:T(1,128)} %fusion.72.refs_2_, ...), custom_call_target="tpu_custom_call" | custom-call | bytes 65536 | tf_op jit(solution)/shard_map/attend_back1/pallas_call | solution.py:135
  981.5 17.9 %collective-permute-done.53 = bf16[2,128,2048]{2,1,0:T(8,128)(2,1)S(1)} collective-permute-done((bf16[2,128,2048]{2,1,0:T(8,128)(2,1)S(1)}, bf16[2,128,2048]{2,1,0:T(8,128)(2,1)S(1)}, u32[]{:S(2)}, u32[]{:S(2)}) %collective-permute-start.53) | collective-permute-done | bytes 1048608 | tf_op jit(solution)/shard_map/ppermute | solution.py:163
  1022.0 19.3 %collective-permute-done.55.refs_8_ = bf16[128,2048]{1,0:T(8,128)(2,1)} collective-permute-done((bf16[128,2048]{1,0:T(8,128)(2,1)}, bf16[128,2048]{1,0:T(8,128)(2,1)}, u32[]{:S(2)}, u32[]{:S(2)}) %collective-permute-start.55) | collective-permute-done | bytes 524320 | tf_op jit(solution)/shard_map/ppermute | solution.py:172
  1052.1 19.4 %collective-permute-done.57 = bf16[1024,1536]{1,0:T(8,128)(2,1)} collective-permute-done((bf16[1024,1536]{1,0:T(8,128)(2,1)}, bf16[1024,1536]{1,0:T(8,128)(2,1)}, u32[]{:S(2)}, u32[]{:S(2)}) %collective-permute-start.57) | collective-permute-done | bytes 3145760 | tf_op jit(solution)/shard_map/ppermute | solution.py:167
  1100.8 13.6 %collective-permute-start.67 = (f32[33,128]{1,0:T(8,128)S(1)}, f32[33,128]{1,0:T(8,128)S(1)}, u32[]{:S(2)}, u32[]{:S(2)}) collective-permute-start(f32[33,128]{1,0:T(8,128)S(1)} %add.554), channel_id=1, source_target_pairs={{0,4},{4,0},{8,12},{12,8},{1,5},{5,1},{9,13},{13,9},{2,6},{6,2},{1... | collective-permute-start | bytes 50696 | tf_op jit(solution)/shard_map/ppermute | solution.py:296
  1142.3 24.9 %reduce-scatter.12.cloned.1.call-done = bf16[256,1536]{1,0:T(8,128)(2,1)} async-done(((bf16[1024,1536]{1,0:T(8,128)(2,1)}), bf16[256,1536]{1,0:T(8,128)(2,1)}) %reduce-scatter.12.cloned.1.call-update) | async-done | bytes 786448 | tf_op jit(solution)/shard_map/reduce_scatter | solution.py:645
  (712 shorter events, 662.9 us)
Async XLA Ops:
  7.2 65.2 %all-gather.9.cloned.1.call-start = ((), (), s32[]{:S(2)}) async-start(), calls=%async_computation.5 | async-start | bytes 1392640 | tf_op jit(solution)/shard_map/all_gather | solution.py:375
  10.3 100.5 %all-gather.11.cloned.1.call-start = ((), (), s32[]{:S(2)}) async-start(), calls=%async_computation.6 | async-start | bytes 1310720 | tf_op jit(solution)/shard_map/all_gather | solution.py:375
  17.8 54.5 %collective-permute-start.1 = (bf16[128,2048]{1,0:T(8,128)(2,1)S(1)}, bf16[128,2048]{1,0:T(8,128)(2,1)S(1)}, u32[]{:S(2)}, u32[]{:S(2)}) collective-permute-start(bf16[128,2048]{1,0:T(8,128)(2,1)S(1)} %get-tuple-element.324), channel_id=1, source_target_pairs={{0,8},{4,12},{8,0},{12,4},{1,9},{5,13},{9,1},{13,5},{2,10},{6,14},... | collective-permute-start | bytes 1572872 | tf_op jit(solution)/shard_map/ppermute | solution.py:172
  20.4 51.9 %collective-permute-start.2 = (bf16[128,2048]{1,0:T(8,128)(2,1)S(1)}, bf16[128,2048]{1,0:T(8,128)(2,1)S(1)}, u32[]{:S(2)}, u32[]{:S(2)}) collective-permute-start(bf16[128,2048]{1,0:T(8,128)(2,1)S(1)} %get-tuple-element.323), channel_id=1, source_target_pairs={{0,12},{4,0},{8,4},{12,8},{1,13},{5,1},{9,5},{13,9},{2,14},{6,2},{... | collective-permute-start | bytes 1572872 | tf_op jit(solution)/shard_map/ppermute | solution.py:172
  72.3 77.4 %all-gather.15.cloned.1.call-start = ((), (), s32[]{:S(2)}) async-start(), calls=%async_computation.8 | async-start | bytes 1310720 | tf_op jit(solution)/shard_map/all_gather | solution.py:375
  73.0 114.4 %all-gather.13.cloned.1.call-start = ((), (), s32[]{:S(2)}) async-start(), calls=%async_computation.7 | async-start | bytes 1310720 | tf_op jit(solution)/shard_map/all_gather | solution.py:375
  110.8 144.6 %all-gather.17.cloned.1.call-start = ((), (), s32[]{:S(2)}) async-start(), calls=%async_computation.9 | async-start | bytes 3522560 | tf_op jit(solution)/shard_map/all_gather | solution.py:375
  115.0 177.8 %collective-permute-start.27 = (bf16[256,1376]{0,1:T(8,128)(2,1)}, bf16[256,1376]{0,1:T(8,128)(2,1)}, u32[]{:S(2)}, u32[]{:S(2)}) collective-permute-start(bf16[256,1376]{0,1:T(8,128)(2,1)} %bitcast.323), channel_id=1, source_target_pairs={{0,16},{16,0},{1,17},{17,1},{2,18},{18,2},{3,19},{19,3},{4,20},{20... | collective-permute-start | bytes 2113544 | tf_op jit(solution)/shard_map/ppermute | solution.py:167
  149.8 155.7 %all-gather.19.cloned.1.call-start = ((), (), s32[]{:S(2)}) async-start(), calls=%async_computation.10 | async-start | bytes 3522560 | tf_op jit(solution)/shard_map/all_gather | solution.py:375
  187.4 232.9 %all-gather.21.cloned.1.call-start = ((), (), s32[]{:S(2)}) async-start(), calls=%async_computation.11 | async-start | bytes 3522560 | tf_op jit(solution)/shard_map/all_gather | solution.py:378
  255.5 176.8 %all-gather.23.cloned.1.call-start = ((), (), s32[]{:S(2)}) async-start(), calls=%async_computation.12 | async-start | bytes 3522560 | tf_op jit(solution)/shard_map/all_gather | solution.py:378
  290.8 64.3 %collective-permute-start.18 = (bf16[1024,1376]{0,1:T(8,128)(2,1)}, bf16[1024,1376]{0,1:T(8,128)(2,1)}, u32[]{:S(2)}, u32[]{:S(2)}) collective-permute-start(bf16[1024,1376]{0,1:T(8,128)(2,1)} %all-gather.17.cloned.1.call-done), channel_id=1, source_target_pairs={{0,16},{16,0},{1,17},{17,1},{2,18},{18,2},{3,19},{19,3},{4,20},{20... | collective-permute-start | bytes 8454152 | tf_op jit(solution)/shard_map/ppermute | solution.py:167
  292.8 491.6 %reduce-scatter.6.cloned.1.call-start = ((), (), s32[]{:S(2)}) async-start(), calls=%async_computation.13 | async-start | bytes 6340608 | tf_op jit(solution)/shard_map/reduce_scatter | solution.py:250
  305.4 108.9 %collective-permute-start.23 = (bf16[1024,1376]{0,1:T(8,128)(2,1)}, bf16[1024,1376]{0,1:T(8,128)(2,1)S(1)}, u32[]{:S(2)}, u32[]{:S(2)}) collective-permute-start(bf16[1024,1376]{0,1:T(8,128)(2,1)} %all-gather.19.cloned.1.call-done), channel_id=1, source_target_pairs={{0,16},{16,0},{1,17},{17,1},{2,18},{18,2},{3,19},{19,3},{4,20},{20... | collective-permute-start | bytes 8454152 | tf_op jit(solution)/shard_map/ppermute | solution.py:167
  360.9 56.1 %collective-permute-start.22 = (bf16[2,128,2048]{2,1,0:T(8,128)(2,1)S(1)}, bf16[2,128,2048]{2,1,0:T(8,128)(2,1)S(1)}, u32[]{:S(2)}, u32[]{:S(2)}) collective-permute-start(bf16[2,128,2048]{2,1,0:T(8,128)(2,1)S(1)} %multiply_convert_fusion.6), channel_id=1, source_target_pairs={{0,2},{1,3},{2,0},{3,1},{4,6},{5,7},{6,4},{7,5},{8,10},{9,11},{10,... | collective-permute-start | bytes 3145736 | tf_op jit(solution)/shard_map/ppermute | solution.py:163
  386.9 66.2 %collective-permute-start.24 = (bf16[128,2048]{1,0:T(8,128)(2,1)}, bf16[128,2048]{1,0:T(8,128)(2,1)}, u32[]{:S(2)}, u32[]{:S(2)}) collective-permute-start(bf16[128,2048]{1,0:T(8,128)(2,1)} %get-tuple-element.317), channel_id=1, source_target_pairs={{0,4},{4,8},{8,12},{12,0},{1,5},{5,9},{9,13},{13,1},{2,6},{6,10},{... | collective-permute-start | bytes 1572872 | tf_op jit(solution)/shard_map/ppermute | solution.py:172
  388.2 64.8 %collective-permute-start.25 = (bf16[128,2048]{1,0:T(8,128)(2,1)}, bf16[128,2048]{1,0:T(8,128)(2,1)}, u32[]{:S(2)}, u32[]{:S(2)}) collective-permute-start(bf16[128,2048]{1,0:T(8,128)(2,1)} %get-tuple-element.316), channel_id=1, source_target_pairs={{0,8},{4,12},{8,0},{12,4},{1,9},{5,13},{9,1},{13,5},{2,10},{6,14},... | collective-permute-start | bytes 1572872 | tf_op jit(solution)/shard_map/ppermute | solution.py:172
  668.3 281.0 %reduce-scatter.8.cloned.1.call-start = ((), (), s32[]{:S(2)}) async-start(), calls=%async_computation.14 | async-start | bytes 6340608 | tf_op jit(solution)/shard_map/reduce_scatter | solution.py:250
  822.6 257.1 %reduce-scatter.10.cloned.1.call-start = ((), (), s32[]{:S(2)}) async-start(), calls=%async_computation.15 | async-start | bytes 6340608 | tf_op jit(solution)/shard_map/reduce_scatter | solution.py:250
  921.8 204.0 %reduce-scatter.14.cloned.1.call-start = ((), (), s32[]{:S(2)}) async-start(), calls=%async_computation.17 | async-start | bytes 1310720 | tf_op jit(solution)/shard_map/reduce_scatter | solution.py:536
  978.6 92.9 %collective-permute-start.57 = (bf16[1024,1536]{1,0:T(8,128)(2,1)}, bf16[1024,1536]{1,0:T(8,128)(2,1)}, u32[]{:S(2)}, u32[]{:S(2)}) collective-permute-start(bf16[1024,1536]{1,0:T(8,128)(2,1)} %add_convert_fusion.4), channel_id=1, source_target_pairs={{0,16},{16,0},{1,17},{17,1},{2,18},{18,2},{3,19},{19,3},{4,20},{20... | collective-permute-start | bytes 9437192 | tf_op jit(solution)/shard_map/ppermute | solution.py:167
  1012.6 67.1 %collective-permute-start.60 = (bf16[128,2048]{1,0:T(8,128)(2,1)S(1)}, bf16[128,2048]{1,0:T(8,128)(2,1)}, u32[]{:S(2)}, u32[]{:S(2)}) collective-permute-start(bf16[128,2048]{1,0:T(8,128)(2,1)S(1)} %get-tuple-element.189.refs_0_), channel_id=1, source_target_pairs={{0,2},{1,3},{2,0},{3,1},{4,6},{5,7},{6,4},{7,5},{8,10},{9,11},{10,... | collective-permute-start | bytes 1572872 | tf_op jit(solution)/shard_map/ppermute | solution.py:163
  1014.1 153.1 %reduce-scatter.12.cloned.1.call-start = ((), (), s32[]{:S(2)}) async-start(), calls=%async_computation.16 | async-start | bytes 3932160 | tf_op jit(solution)/shard_map/reduce_scatter | solution.py:645
  1020.4 59.3 %collective-permute-start.61 = (bf16[128,2048]{1,0:T(8,128)(2,1)}, bf16[128,2048]{1,0:T(8,128)(2,1)}, u32[]{:S(2)}, u32[]{:S(2)}) collective-permute-start(bf16[128,2048]{1,0:T(8,128)(2,1)} %collective-permute-done.54.refs_4_), channel_id=1, source_target_pairs={{0,2},{1,3},{2,0},{3,1},{4,6},{5,7},{6,4},{7,5},{8,10},{9,11},{10,... | collective-permute-start | bytes 1572872 | tf_op jit(solution)/shard_map/ppermute | solution.py:163
  (222 other events, 3490.6 us)
Sparse Core Ops, SparseCore 0:
  10.4 59.9 all-gather.8
  72.4 38.2 all-gather.10
  112.3 27.4 all-gather.14
  141.2 29.6 all-gather.12
  172.3 56.3 all-gather.16
  230.2 56.2 all-gather.18
  288.0 56.2 all-gather.20
  345.8 86.3 all-gather.22
  668.4 116.0 reduce-scatter.5
  822.8 116.4 reduce-scatter.7
  942.9 133.2 reduce-scatter.9
  1078.9 26.2 reduce-scatter.13
  1107.5 59.6 reduce-scatter.11

commit v3 on v2

--- a/solution.py
+++ b/solution.py
@@ -390,7 +390,7 @@
     w_query, w_key, w_value, w_out, w_gate, w_up = [
         jnp.concatenate(pair, axis=0) for pair in fetched
     ]
-    teacher_parts = own_part(after(teacher, part_up))
+    teacher_parts = own_part(after(teacher, part_down[1]))
     target = by_chunk(teacher_parts)
     per = 2
     pairs = range(n_chunk // per)
@@ -457,8 +457,8 @@
         attention(p)
         sent[p], kept[p] = order(lambda a: split_part(right_dot(a, w_out), per), attended[p])
     pass_core(0)
+    order.wait(fetched[4][1])
     pass_core(1)
-    order.wait(fetched[4][1])
     low = [enter_feed(0)]
     order.wait(part_up)
     low.append(enter_feed(1))

time: 1190 us -> 1220 us (1.025)
  waiting for transfers between devices: 489 us -> 515 us
    ppermute x10, waiting for transfers between devices: 114 us -> 55.3 us  [dp_swap(): return lax.ppermute(v, 'dp', [(i, i ^ 1) for i in range(2)])]
    all_gather x2, waiting for transfers between devices: 8.26 us -> 54.6 us  [slot_device(): lax.all_gather(v, 'ctx', axis=0, tiled=True)]
    ppermute x24, waiting for transfers between devices: 136 us -> 162 us  [chip_swap(): return lax.ppermute(v, 'mp', [(i, i ^ 2) for i in range(4)])]
    all_gather x6, waiting for transfers between devices: 36.1 us -> 50.5 us  [slot_device(): parts.append(lax.all_gather(shard, 'ctx', axis=0, tiled=True))]
    unnamed x327 -> x321, local copies, waits for them, and re-layouts: 45.1 us -> 47.4 us
where the time goes in v3:
time: 1220 us
  waiting for transfers between devices  515 us (42%)
  matrix products  290 us (24%)
  other arithmetic  118 us (10%)
  local copies, waits for them, and re-layouts  101 us (8%)
  starting transfers between devices  87.1 us (7%)
  Pallas kernels  85.6 us (7%)
  between operations  20.3 us (2%)
    dot_general x42, matrix products, dot_t(): return lax.dot_general(a, b, (dims, ((), ())), preferred_element_type=F32)  290 us
    ppermute x24, waiting for transfers between devices, chip_swap(): return lax.ppermute(v, 'mp', [(i, i ^ 2) for i in range(4)])  162 us
    ppermute x12, waiting for transfers between devices, ctx_turn(): return lax.ppermute(v, 'ctx', [(i, (i + steps) % n) for i in range(n)])  110 us
    pallas_call x4, Pallas kernels, attend_call(): pl.pallas_call(lambda *refs: kernel(pair, per, back, *refs), grid_spec=pl...  67.4 us
    ppermute x10, waiting for transfers between devices, dp_swap(): return lax.ppermute(v, 'dp', [(i, i ^ 1) for i in range(2)])  55.3 us
    all_gather x2, waiting for transfers between devices, slot_device(): lax.all_gather(v, 'ctx', axis=0, tiled=True)  54.6 us
    all_gather x6, waiting for transfers between devices, slot_device(): parts.append(lax.all_gather(shard, 'ctx', axis=0, tiled=True))  50.5 us
    unnamed x321, local copies, waits for them, and re-layouts  47.4 us
  transfers between devices with their start and end apart: 90, of which 38 were waited for; matrix products, arithmetic and copies ran while one was open for 36% of the time, Pallas kernels for 7%

profile of v3, /device:TPU:0, one launch (start us, length us, event | category | flops | bytes accessed | tf_op | source)
XLA Modules:
  0.0 1216.3 jit_solution(10110656802699902983)
XLA Ops:
  10.3 16.0 %collective-permute-done.24 = bf16[256,1376]{0,1:T(8,128)(2,1)S(1)} collective-permute-done((bf16[256,1376]{0,1:T(8,128)(2,1)}, bf16[256,1376]{0,1:T(8,128)(2,1)S(1)}, u32[]{:S(2)}, u32[]{:S(2)}) %collective-permute-start.24) | collective-permute-done | bytes 704544 | tf_op jit(solution)/shard_map/ppermute | solution.py:167
  32.2 54.6 %all-gather.21.cloned.1.call-done = bf16[1024,1376]{0,1:T(8,128)(2,1)} async-done(((bf16[256,1376]{0,1:T(8,128)(2,1)}), bf16[1024,1376]{0,1:T(8,128)(2,1)}) %all-gather.21.cloned.1.call-update) | async-done | bytes 2818064 | tf_op jit(solution)/shard_map/all_gather | solution.py:378
  97.0 23.4 %collective-permute-done = bf16[128,2048]{1,0:T(8,128)(2,1)S(1)} collective-permute-done((bf16[128,2048]{1,0:T(8,128)(2,1)S(1)}, bf16[128,2048]{1,0:T(8,128)(2,1)S(1)}, u32[]{:S(2)}, u32[]{:S(2)}) %collective-permute-start) | collective-permute-done | bytes 524320 | tf_op jit(solution)/shard_map/ppermute | solution.py:172
  120.4 28.9 %collective-permute-done.1 = bf16[128,2048]{1,0:T(8,128)(2,1)S(1)} collective-permute-done((bf16[128,2048]{1,0:T(8,128)(2,1)S(1)}, bf16[128,2048]{1,0:T(8,128)(2,1)S(1)}, u32[]{:S(2)}, u32[]{:S(2)}) %collective-permute-start.1) | collective-permute-done | bytes 524320 | tf_op jit(solution)/shard_map/ppermute | solution.py:172
  153.4 10.8 collective-permute-done.3
  249.1 13.3 %collective-permute-done.12 = bf16[1024,512]{1,0:T(8,128)(2,1)} collective-permute-done((bf16[1024,512]{1,0:T(8,128)(2,1)}, bf16[1024,512]{1,0:T(8,128)(2,1)}, u32[]{:S(2)}, u32[]{:S(2)}) %collective-permute-start.12) | collective-permute-done | bytes 1048608 | tf_op jit(solution)/shard_map/ppermute | solution.py:167
  314.4 16.5 %attend1.1 = (bf16[1024,512]{1,0:T(8,128)(2,1)}, f32[4,2,512]{2,1,0:T(2,128)}) custom-call(s32[1]{0:T(128)} %bitcast.31.refs_0_, s32[512,1]{1,0:T(8,128)} %fusion.62.refs_1_, s32[1,512]{1,0:T(1,128)} %fusion.72.refs_2_, bf16[1024,512]{1,0:T(8,128)(2,1)} %convolution_convert_fusion.4.refs_3_, bf16[1024,512]{1,0:T(8,128)(2,1)} %convolution_convert_fusion.6.refs_4_.refs_6_, ...), custom_call_target="tpu_custom_call" | custom-call | flops 19327352832 | bytes 7340032 | tf_op jit(solution)/shard_map/attend1/pallas_call | solution.py:135
  350.3 43.1 %all-gather.19.cloned.1.call-done = bf16[1024,1376]{0,1:T(8,128)(2,1)} async-done(((bf16[256,1376]{0,1:T(8,128)(2,1)}), bf16[1024,1376]{0,1:T(8,128)(2,1)}) %all-gather.19.cloned.1.call-update) | async-done | bytes 2818064 | tf_op jit(solution)/shard_map/all_gather | solution.py:375
  403.9 20.5 %collective-permute-done.20 = bf16[2,128,2048]{2,1,0:T(8,128)(2,1)S(1)} collective-permute-done((bf16[2,128,2048]{2,1,0:T(8,128)(2,1)S(1)}, bf16[2,128,2048]{2,1,0:T(8,128)(2,1)S(1)}, u32[]{:S(2)}, u32[]{:S(2)}) %collective-permute-start.20) | collective-permute-done | bytes 1048608 | tf_op jit(solution)/shard_map/ppermute | solution.py:163
  426.2 19.5 %collective-permute-done.19 = bf16[2,128,2048]{2,1,0:T(8,128)(2,1)S(1)} collective-permute-done((bf16[2,128,2048]{2,1,0:T(8,128)(2,1)S(1)}, bf16[2,128,2048]{2,1,0:T(8,128)(2,1)S(1)}, u32[]{:S(2)}, u32[]{:S(2)}) %collective-permute-start.19) | collective-permute-done | bytes 1048608 | tf_op jit(solution)/shard_map/ppermute | solution.py:163
  565.7 19.4 %collective-permute-done.33 = bf16[2,128,2048]{2,1,0:T(8,128)(2,1)S(1)} collective-permute-done((bf16[2,128,2048]{2,1,0:T(8,128)(2,1)S(1)}, bf16[2,128,2048]{2,1,0:T(8,128)(2,1)S(1)}, u32[]{:S(2)}, u32[]{:S(2)}) %collective-permute-start.33) | collective-permute-done | bytes 1048608 | tf_op jit(solution)/shard_map/ppermute | solution.py:163
  589.9 12.0 multiply_convert_fusion.2
  655.2 21.5 %collective-permute-done.39 = bf16[128,2048]{1,0:T(8,128)(2,1)S(1)} collective-permute-done((bf16[128,2048]{1,0:T(8,128)(2,1)S(1)}, bf16[128,2048]{1,0:T(8,128)(2,1)S(1)}, u32[]{:S(2)}, u32[]{:S(2)}) %collective-permute-start.39) | collective-permute-done | bytes 524320 | tf_op jit(solution)/shard_map/ppermute | solution.py:172
  682.5 12.0 multiply_convert_fusion
  747.4 10.8 add_convert_fusion.1
  766.6 14.8 %attend_back0.1 = (bf16[1024,512]{1,0:T(8,128)(2,1)}, f32[1024,512]{1,0:T(8,128)}, f32[1024,512]{1,0:T(8,128)}) custom-call(s32[1]{0:T(128)} %bitcast.31.refs_0_, s32[512,1]{1,0:T(8,128)} %fusion.62.refs_1_, s32[1,512]{1,0:T(1,128)} %fusion.72.refs_2_, bf16[1024,512]{1,0:T(8,128)(2,1)} %convolution_convert_fusion.7.refs_3_, ...), custom_call_target="tpu_custom_call" | custom-call | bytes 65536 | tf_op jit(solution)/shard_map/attend_back0/pallas_call | solution.py:135
  784.1 39.5 %reduce-scatter.6.cloned.1.call-done = bf16[256,1376]{0,1:T(8,128)(2,1)} async-done(((bf16[2048,1376]{0,1:T(8,128)(2,1)}), bf16[256,1376]{0,1:T(8,128)(2,1)}) %reduce-scatter.6.cloned.1.call-update) | async-done | bytes 704528 | tf_op jit(solution)/shard_map/reduce_scatter | solution.py:250
  832.3 23.3 %collective-permute-done.46 = bf16[2,128,2048]{2,1,0:T(8,128)(2,1)S(1)} collective-permute-done((bf16[2,128,2048]{2,1,0:T(8,128)(2,1)S(1)}, bf16[2,128,2048]{2,1,0:T(8,128)(2,1)S(1)}, u32[]{:S(2)}, u32[]{:S(2)}) %collective-permute-start.46) | collective-permute-done | bytes 1048608 | tf_op jit(solution)/shard_map/ppermute | solution.py:163
  899.2 25.4 %attend_back1.1 = (bf16[1024,512]{1,0:T(8,128)(2,1)}, bf16[1024,512]{1,0:T(8,128)(2,1)}, bf16[1024,512]{1,0:T(8,128)(2,1)}, bf16[1024,512]{1,0:T(8,128)(2,1)}, bf16[1024,512]{1,0:T(8,128)(2,1)}) custom-call(s32[1]{0:T(128)} %bitcast.31.refs_0_, s32[512,1]{1,0:T(8,128)} %fusion.62.refs_1_, s32[1,512]{1,0:T(1,128)} %fusion.72.refs_2_, ...), custom_call_target="tpu_custom_call" | custom-call | bytes 65536 | tf_op jit(solution)/shard_map/attend_back1/pallas_call | solution.py:135
  1020.4 18.1 %collective-permute-done.53 = bf16[2,128,2048]{2,1,0:T(8,128)(2,1)S(1)} collective-permute-done((bf16[2,128,2048]{2,1,0:T(8,128)(2,1)S(1)}, bf16[2,128,2048]{2,1,0:T(8,128)(2,1)S(1)}, u32[]{:S(2)}, u32[]{:S(2)}) %collective-permute-start.53) | collective-permute-done | bytes 1048608 | tf_op jit(solution)/shard_map/ppermute | solution.py:163
  1060.9 19.4 %collective-permute-done.55.refs_8_ = bf16[128,2048]{1,0:T(8,128)(2,1)} collective-permute-done((bf16[128,2048]{1,0:T(8,128)(2,1)}, bf16[128,2048]{1,0:T(8,128)(2,1)}, u32[]{:S(2)}, u32[]{:S(2)}) %collective-permute-start.55) | collective-permute-done | bytes 524320 | tf_op jit(solution)/shard_map/ppermute | solution.py:172
  1091.1 19.4 %collective-permute-done.57 = bf16[1024,1536]{1,0:T(8,128)(2,1)} collective-permute-done((bf16[1024,1536]{1,0:T(8,128)(2,1)}, bf16[1024,1536]{1,0:T(8,128)(2,1)}, u32[]{:S(2)}, u32[]{:S(2)}) %collective-permute-start.57) | collective-permute-done | bytes 3145760 | tf_op jit(solution)/shard_map/ppermute | solution.py:167
  1139.8 13.1 %collective-permute-start.67 = (f32[33,128]{1,0:T(8,128)S(1)}, f32[33,128]{1,0:T(8,128)S(1)}, u32[]{:S(2)}, u32[]{:S(2)}) collective-permute-start(f32[33,128]{1,0:T(8,128)S(1)} %add.554), channel_id=1, source_target_pairs={{0,4},{4,0},{8,12},{12,8},{1,5},{5,1},{9,13},{13,9},{2,6},{6,2},{1... | collective-permute-start | bytes 50696 | tf_op jit(solution)/shard_map/ppermute | solution.py:296
  1181.3 24.8 %reduce-scatter.12.cloned.1.call-done = bf16[256,1536]{1,0:T(8,128)(2,1)} async-done(((bf16[1024,1536]{1,0:T(8,128)(2,1)}), bf16[256,1536]{1,0:T(8,128)(2,1)}) %reduce-scatter.12.cloned.1.call-update) | async-done | bytes 786448 | tf_op jit(solution)/shard_map/reduce_scatter | solution.py:645
  (700 shorter events, 675.8 us)
Async XLA Ops:
  7.2 79.6 %all-gather.21.cloned.1.call-start = ((), (), s32[]{:S(2)}) async-start(), calls=%async_computation.11 | async-start | bytes 3522560 | tf_op jit(solution)/shard_map/all_gather | solution.py:378
  27.1 139.0 %all-gather.9.cloned.1.call-start = ((), (), s32[]{:S(2)}) async-start(), calls=%async_computation.5 | async-start | bytes 1392640 | tf_op jit(solution)/shard_map/all_gather | solution.py:375
  30.2 177.1 %all-gather.11.cloned.1.call-start = ((), (), s32[]{:S(2)}) async-start(), calls=%async_computation.6 | async-start | bytes 1310720 | tf_op jit(solution)/shard_map/all_gather | solution.py:375
  93.1 56.1 %collective-permute-start.1 = (bf16[128,2048]{1,0:T(8,128)(2,1)S(1)}, bf16[128,2048]{1,0:T(8,128)(2,1)S(1)}, u32[]{:S(2)}, u32[]{:S(2)}) collective-permute-start(bf16[128,2048]{1,0:T(8,128)(2,1)S(1)} %get-tuple-element.324), channel_id=1, source_target_pairs={{0,8},{4,12},{8,0},{12,4},{1,9},{5,13},{9,1},{13,5},{2,10},{6,14},... | collective-permute-start | bytes 1572872 | tf_op jit(solution)/shard_map/ppermute | solution.py:172
  94.2 55.1 %collective-permute-start.2 = (bf16[128,2048]{1,0:T(8,128)(2,1)S(1)}, bf16[128,2048]{1,0:T(8,128)(2,1)S(1)}, u32[]{:S(2)}, u32[]{:S(2)}) collective-permute-start(bf16[128,2048]{1,0:T(8,128)(2,1)S(1)} %get-tuple-element.323), channel_id=1, source_target_pairs={{0,12},{4,0},{8,4},{12,8},{1,13},{5,1},{9,5},{13,9},{2,14},{6,2},{... | collective-permute-start | bytes 1572872 | tf_op jit(solution)/shard_map/ppermute | solution.py:172
  149.3 65.5 %all-gather.15.cloned.1.call-start = ((), (), s32[]{:S(2)}) async-start(), calls=%async_computation.8 | async-start | bytes 1310720 | tf_op jit(solution)/shard_map/all_gather | solution.py:375
  167.7 100.4 %all-gather.13.cloned.1.call-start = ((), (), s32[]{:S(2)}) async-start(), calls=%async_computation.7 | async-start | bytes 1310720 | tf_op jit(solution)/shard_map/all_gather | solution.py:375
  207.4 105.5 %all-gather.17.cloned.1.call-start = ((), (), s32[]{:S(2)}) async-start(), calls=%async_computation.9 | async-start | bytes 3522560 | tf_op jit(solution)/shard_map/all_gather | solution.py:375
  232.6 160.8 %all-gather.19.cloned.1.call-start = ((), (), s32[]{:S(2)}) async-start(), calls=%async_computation.10 | async-start | bytes 3522560 | tf_op jit(solution)/shard_map/all_gather | solution.py:375
  286.3 170.8 %all-gather.23.cloned.1.call-start = ((), (), s32[]{:S(2)}) async-start(), calls=%async_computation.12 | async-start | bytes 3522560 | tf_op jit(solution)/shard_map/all_gather | solution.py:378
  312.9 81.6 %collective-permute-start.18 = (bf16[1024,1376]{0,1:T(8,128)(2,1)}, bf16[1024,1376]{0,1:T(8,128)(2,1)}, u32[]{:S(2)}, u32[]{:S(2)}) collective-permute-start(bf16[1024,1376]{0,1:T(8,128)(2,1)} %all-gather.17.cloned.1.call-done), channel_id=1, source_target_pairs={{0,16},{16,0},{1,17},{17,1},{2,18},{18,2},{3,19},{19,3},{4,20},{20... | collective-permute-start | bytes 8454152 | tf_op jit(solution)/shard_map/ppermute | solution.py:167
  336.2 57.3 %collective-permute-start.17 = (bf16[2,256,2048]{2,1,0:T(8,128)(2,1)}, bf16[2,256,2048]{2,1,0:T(8,128)(2,1)}, u32[]{:S(2)}, u32[]{:S(2)}) collective-permute-start(bf16[2,256,2048]{2,1,0:T(8,128)(2,1)} %slice.578), channel_id=1, source_target_pairs={{0,1},{1,0},{2,3},{3,2},{4,5},{5,4},{6,7},{7,6},{8,9},{9,8},{10,11... | collective-permute-start | bytes 6291464 | tf_op jit(solution)/shard_map/ppermute | solution.py:159
  340.7 158.5 %collective-permute-start.25 = (bf16[128,2048]{1,0:T(8,128)(2,1)}, bf16[128,2048]{1,0:T(8,128)(2,1)}, u32[]{:S(2)}, u32[]{:S(2)}) collective-permute-start(bf16[128,2048]{1,0:T(8,128)(2,1)} %get-tuple-element.317), channel_id=1, source_target_pairs={{0,4},{4,8},{8,12},{12,0},{1,5},{5,9},{9,13},{13,1},{2,6},{6,10},{... | collective-permute-start | bytes 1572872 | tf_op jit(solution)/shard_map/ppermute | solution.py:172
  346.9 152.3 %collective-permute-start.26 = (bf16[128,2048]{1,0:T(8,128)(2,1)}, bf16[128,2048]{1,0:T(8,128)(2,1)}, u32[]{:S(2)}, u32[]{:S(2)}) collective-permute-start(bf16[128,2048]{1,0:T(8,128)(2,1)} %get-tuple-element.316), channel_id=1, source_target_pairs={{0,8},{4,12},{8,0},{12,4},{1,9},{5,13},{9,1},{13,5},{2,10},{6,14},... | collective-permute-start | bytes 1572872 | tf_op jit(solution)/shard_map/ppermute | solution.py:172
  348.3 51.5 %collective-permute-start.16 = (bf16[2,128,2048]{2,1,0:T(8,128)(2,1)S(1)}, bf16[2,128,2048]{2,1,0:T(8,128)(2,1)}, u32[]{:S(2)}, u32[]{:S(2)}) collective-permute-start(bf16[2,128,2048]{2,1,0:T(8,128)(2,1)S(1)} %slice.587), channel_id=1, source_target_pairs={{0,2},{1,3},{2,0},{3,1},{4,6},{5,7},{6,4},{7,5},{8,10},{9,11},{10,... | collective-permute-start | bytes 3145736 | tf_op jit(solution)/shard_map/ppermute | solution.py:163
  350.2 473.4 %reduce-scatter.6.cloned.1.call-start = ((), (), s32[]{:S(2)}) async-start(), calls=%async_computation.13 | async-start | bytes 6340608 | tf_op jit(solution)/shard_map/reduce_scatter | solution.py:250
  393.4 66.6 %collective-permute-start.23 = (bf16[1024,1376]{0,1:T(8,128)(2,1)}, bf16[1024,1376]{0,1:T(8,128)(2,1)}, u32[]{:S(2)}, u32[]{:S(2)}) collective-permute-start(bf16[1024,1376]{0,1:T(8,128)(2,1)} %all-gather.19.cloned.1.call-done), channel_id=1, source_target_pairs={{0,16},{16,0},{1,17},{17,1},{2,18},{18,2},{3,19},{19,3},{4,20},{20... | collective-permute-start | bytes 8454152 | tf_op jit(solution)/shard_map/ppermute | solution.py:167
  708.1 280.1 %reduce-scatter.8.cloned.1.call-start = ((), (), s32[]{:S(2)}) async-start(), calls=%async_computation.14 | async-start | bytes 6340608 | tf_op jit(solution)/shard_map/reduce_scatter | solution.py:250
  861.8 256.9 %reduce-scatter.10.cloned.1.call-start = ((), (), s32[]{:S(2)}) async-start(), calls=%async_computation.15 | async-start | bytes 6340608 | tf_op jit(solution)/shard_map/reduce_scatter | solution.py:250
  960.5 204.3 %reduce-scatter.14.cloned.1.call-start = ((), (), s32[]{:S(2)}) async-start(), calls=%async_computation.17 | async-start | bytes 1310720 | tf_op jit(solution)/shard_map/reduce_scatter | solution.py:536
  1017.5 93.0 %collective-permute-start.57 = (bf16[1024,1536]{1,0:T(8,128)(2,1)}, bf16[1024,1536]{1,0:T(8,128)(2,1)}, u32[]{:S(2)}, u32[]{:S(2)}) collective-permute-start(bf16[1024,1536]{1,0:T(8,128)(2,1)} %add_convert_fusion.4), channel_id=1, source_target_pairs={{0,16},{16,0},{1,17},{17,1},{2,18},{18,2},{3,19},{19,3},{4,20},{20... | collective-permute-start | bytes 9437192 | tf_op jit(solution)/shard_map/ppermute | solution.py:167
  1051.5 67.2 %collective-permute-start.60 = (bf16[128,2048]{1,0:T(8,128)(2,1)S(1)}, bf16[128,2048]{1,0:T(8,128)(2,1)}, u32[]{:S(2)}, u32[]{:S(2)}) collective-permute-start(bf16[128,2048]{1,0:T(8,128)(2,1)S(1)} %get-tuple-element.189.refs_0_), channel_id=1, source_target_pairs={{0,2},{1,3},{2,0},{3,1},{4,6},{5,7},{6,4},{7,5},{8,10},{9,11},{10,... | collective-permute-start | bytes 1572872 | tf_op jit(solution)/shard_map/ppermute | solution.py:163
  1052.9 153.2 %reduce-scatter.12.cloned.1.call-start = ((), (), s32[]{:S(2)}) async-start(), calls=%async_computation.16 | async-start | bytes 3932160 | tf_op jit(solution)/shard_map/reduce_scatter | solution.py:645
  1059.4 59.3 %collective-permute-start.61 = (bf16[128,2048]{1,0:T(8,128)(2,1)}, bf16[128,2048]{1,0:T(8,128)(2,1)}, u32[]{:S(2)}, u32[]{:S(2)}) collective-permute-start(bf16[128,2048]{1,0:T(8,128)(2,1)} %collective-permute-done.54.refs_4_), channel_id=1, source_target_pairs={{0,2},{1,3},{2,0},{3,1},{4,6},{5,7},{6,4},{7,5},{8,10},{9,11},{10,... | collective-permute-start | bytes 1572872 | tf_op jit(solution)/shard_map/ppermute | solution.py:163
  (219 other events, 3430.9 us)
Sparse Core Ops, SparseCore 0:
  27.2 59.5 all-gather.20
  89.0 58.3 all-gather.8
  149.4 36.4 all-gather.10
  187.3 27.4 all-gather.14
  216.2 31.0 all-gather.12
  248.7 56.3 all-gather.16
  306.7 86.6 all-gather.18
  395.0 55.7 all-gather.22
  708.2 115.3 reduce-scatter.5
  861.9 116.3 reduce-scatter.7
  982.0 133.0 reduce-scatter.9
  1117.9 26.2 reduce-scatter.13
  1146.5 59.5 reduce-scatter.11

commit v4 on v3

--- a/solution.py
+++ b/solution.py
@@ -377,7 +377,6 @@
     part_down = [
         lax.all_gather(v, "ctx", axis=0, tiled=True) for v in (shard, dp_swap(down_weight.T))
     ]
-    w_down = jnp.concatenate(part_down, axis=0)
     gates = [x_parts, x_peers, x_cores] + [()] * 3
     fetched = [(part, dp_swap(after(part, *gate))) for part, gate in zip(parts, gates)]
     query_parts = [part.reshape(n_chunk, share + 16, cols) for part in fetched[0]]
@@ -390,7 +389,7 @@
     w_query, w_key, w_value, w_out, w_gate, w_up = [
         jnp.concatenate(pair, axis=0) for pair in fetched
     ]
-    teacher_parts = own_part(after(teacher, part_down[1]))
+    teacher_parts = own_part(after(teacher, part_down[0]))
     target = by_chunk(teacher_parts)
     per = 2
     pairs = range(n_chunk // per)
@@ -580,6 +579,7 @@
         gain_a_parts.append(g_gain)
 
     feed(0)
+    w_down = jnp.concatenate([part_down[0], after(part_down[1], hidden[0])], axis=0)
     order.wait(*teacher_parts)
     project_down(0)
     h2.append(gather_rest(low[1]))

time: 1220 us -> 1200 us (0.984)
  waiting for transfers between devices: 515 us -> 479 us
    all_gather x2, waiting for transfers between devices: 54.6 us -> 0.01 us  [slot_device(): lax.all_gather(v, 'ctx', axis=0, tiled=True)]
    ppermute x10, waiting for transfers between devices: 55.3 us -> 107 us  [dp_swap(): return lax.ppermute(v, 'dp', [(i, i ^ 1) for i in range(2)])]
    ppermute x24, waiting for transfers between devices: 162 us -> 142 us  [chip_swap(): return lax.ppermute(v, 'mp', [(i, i ^ 2) for i in range(4)])]
    all_gather x6, waiting for transfers between devices: 50.5 us -> 36.9 us  [slot_device(): parts.append(lax.all_gather(shard, 'ctx', axis=0, tiled=True))]
    unnamed x321 -> x309, local copies, waits for them, and re-layouts: 47.4 us -> 48 us
  transfers between devices with their start and end apart: 90 -> 90, of which waited for: 38 -> 36; matrix products, arithmetic and copies ran while one was open for 36% -> 37% of each run, Pallas kernels for 7% -> 7%
where the time goes in v4:
time: 1200 us
  waiting for transfers between devices  479 us (40%)
  matrix products  296 us (25%)
  other arithmetic  120 us (10%)
  local copies, waits for them, and re-layouts  101 us (8%)
  starting transfers between devices  94.7 us (8%)
  Pallas kernels  85.7 us (7%)
  between operations  20.4 us (2%)
    dot_general x42, matrix products, dot_t(): return lax.dot_general(a, b, (dims, ((), ())), preferred_element_type=F32)  296 us
    ppermute x24, waiting for transfers between devices, chip_swap(): return lax.ppermute(v, 'mp', [(i, i ^ 2) for i in range(4)])  142 us
    ppermute x12, waiting for transfers between devices, ctx_turn(): return lax.ppermute(v, 'ctx', [(i, (i + steps) % n) for i in range(n)])  108 us
    ppermute x10, waiting for transfers between devices, dp_swap(): return lax.ppermute(v, 'dp', [(i, i ^ 1) for i in range(2)])  107 us
    pallas_call x4, Pallas kernels, attend_call(): pl.pallas_call(lambda *refs: kernel(pair, per, back, *refs), grid_spec=pl...  67.5 us
    unnamed x309, local copies, waits for them, and re-layouts  48 us
    reduce_scatter x3, waiting for transfers between devices, both_scatter(): lax.psum_scatter(grad, ('dp', 'ctx'), scatter_dimension=0, tiled=True)  42.1 us
    all_gather x6, waiting for transfers between devices, slot_device(): parts.append(lax.all_gather(shard, 'ctx', axis=0, tiled=True))  36.9 us
  transfers between devices with their start and end apart: 90, of which 36 were waited for; matrix products, arithmetic and copies ran while one was open for 37% of the time, Pallas kernels for 7%

profile of v4, /device:TPU:0, one launch (start us, length us, event | category | flops | bytes accessed | tf_op | source)
XLA Modules:
  0.0 1197.9 jit_solution(3738961568189303276)
XLA Ops:
  21.7 18.3 %collective-permute-done = bf16[128,2048]{1,0:T(8,128)(2,1)S(1)} collective-permute-done((bf16[128,2048]{1,0:T(8,128)(2,1)S(1)}, bf16[128,2048]{1,0:T(8,128)(2,1)S(1)}, u32[]{:S(2)}, u32[]{:S(2)}) %collective-permute-start) | collective-permute-done | bytes 524320 | tf_op jit(solution)/shard_map/ppermute | solution.py:172
  40.0 32.2 %collective-permute-done.1 = bf16[128,2048]{1,0:T(8,128)(2,1)S(1)} collective-permute-done((bf16[128,2048]{1,0:T(8,128)(2,1)S(1)}, bf16[128,2048]{1,0:T(8,128)(2,1)S(1)}, u32[]{:S(2)}, u32[]{:S(2)}) %collective-permute-start.1) | collective-permute-done | bytes 524320 | tf_op jit(solution)/shard_map/ppermute | solution.py:172
  76.7 34.1 %all-gather.11.cloned.1.call-done = bf16[1024,512]{1,0:T(8,128)(2,1)} async-done(((bf16[256,512]{1,0:T(8,128)(2,1)}), bf16[1024,512]{1,0:T(8,128)(2,1)}) %all-gather.11.cloned.1.call-update) | async-done | bytes 1048592 | tf_op jit(solution)/shard_map/all_gather | solution.py:375
  192.2 17.0 %collective-permute-done.13 = bf16[1024,512]{1,0:T(8,128)(2,1)S(1)} collective-permute-done((bf16[1024,512]{1,0:T(8,128)(2,1)S(1)}, bf16[1024,512]{1,0:T(8,128)(2,1)S(1)}, u32[]{:S(2)}, u32[]{:S(2)}) %collective-permute-start.13) | collective-permute-done | bytes 1048608 | tf_op jit(solution)/shard_map/ppermute | solution.py:167
  256.9 16.2 %attend1.1 = (bf16[1024,512]{1,0:T(8,128)(2,1)}, f32[4,2,512]{2,1,0:T(2,128)}) custom-call(s32[1]{0:T(128)} %bitcast.31.refs_0_, s32[512,1]{1,0:T(8,128)} %fusion.62.refs_1_, s32[1,512]{1,0:T(1,128)} %fusion.72.refs_2_, bf16[1024,512]{1,0:T(8,128)(2,1)} %convolution_convert_fusion.4.refs_3_, bf16[1024,512]{1,0:T(8,128)(2,1)} %convolution_convert_fusion.6.refs_4_.refs_6_, ...), custom_call_target="tpu_custom_call" | custom-call | flops 19327352832 | bytes 7340032 | tf_op jit(solution)/shard_map/attend1/pallas_call | solution.py:135
  281.1 53.3 %collective-permute-done.27 = bf16[256,1376]{0,1:T(8,128)(2,1)} collective-permute-done((bf16[256,1376]{0,1:T(8,128)(2,1)S(1)}, bf16[256,1376]{0,1:T(8,128)(2,1)}, u32[]{:S(2)}, u32[]{:S(2)}) %collective-permute-start.27) | collective-permute-done | bytes 704544 | tf_op jit(solution)/shard_map/ppermute | solution.py:167
  351.0 15.3 %collective-permute-done.16 = bf16[2,128,2048]{2,1,0:T(8,128)(2,1)} collective-permute-done((bf16[2,128,2048]{2,1,0:T(8,128)(2,1)S(1)}, bf16[2,128,2048]{2,1,0:T(8,128)(2,1)}, u32[]{:S(2)}, u32[]{:S(2)}) %collective-permute-start.16) | collective-permute-done | bytes 1048608 | tf_op jit(solution)/shard_map/ppermute | solution.py:163
  371.1 17.6 %collective-permute-done.20 = bf16[2,128,2048]{2,1,0:T(8,128)(2,1)S(1)} collective-permute-done((bf16[2,128,2048]{2,1,0:T(8,128)(2,1)S(1)}, bf16[2,128,2048]{2,1,0:T(8,128)(2,1)S(1)}, u32[]{:S(2)}, u32[]{:S(2)}) %collective-permute-start.20) | collective-permute-done | bytes 1048608 | tf_op jit(solution)/shard_map/ppermute | solution.py:163
  390.5 19.4 %collective-permute-done.19 = bf16[2,128,2048]{2,1,0:T(8,128)(2,1)S(1)} collective-permute-done((bf16[2,128,2048]{2,1,0:T(8,128)(2,1)S(1)}, bf16[2,128,2048]{2,1,0:T(8,128)(2,1)S(1)}, u32[]{:S(2)}, u32[]{:S(2)}) %collective-permute-start.19) | collective-permute-done | bytes 1048608 | tf_op jit(solution)/shard_map/ppermute | solution.py:163
  459.5 11.8 multiply_convert_fusion.5
  511.5 12.1 %multiply_convert_fusion.4 = (bf16[1024,1376]{0,1:T(8,128)(2,1)S(1)}, f32[1024,1376]{0,1:T(8,128)}) fusion(f32[1024,1376]{0,1:T(8,128)} %fusion.90, bf16[1024,2048]{1,0:T(8,128)(2,1)S(1)} %bitcast.282, bf16[2048,1376]{0,1:T(8,128)(2,1)} %constant_dynamic-update-slice_fusion.8), kind=kOutput, calls=%fused_computation.25 | convolution fusion | flops 5779816448 | bytes 23920640 | tf_op jit(solution)/shard_map/dot_general | solution.py:18
  540.7 19.4 %collective-permute-done.33 = bf16[2,128,2048]{2,1,0:T(8,128)(2,1)S(1)} collective-permute-done((bf16[2,128,2048]{2,1,0:T(8,128)(2,1)S(1)}, bf16[2,128,2048]{2,1,0:T(8,128)(2,1)S(1)}, u32[]{:S(2)}, u32[]{:S(2)}) %collective-permute-start.33) | collective-permute-done | bytes 1048608 | tf_op jit(solution)/shard_map/ppermute | solution.py:163
  564.9 12.1 %multiply_convert_fusion.2 = (bf16[1024,1376]{0,1:T(8,128)(2,1)}, bf16[1024,1376]{0,1:T(8,128)(2,1)}) fusion(f32[1024,1376]{0,1:T(8,128)} %copy-done.134, f32[1024,1376]{0,1:T(8,128)} %get-tuple-element.342, bf16[1024,2048]{1,0:T(8,128)(2,1)S(1)} %bitcast.290, bf16[2048,1376]{0,1:T(8,128)(2,1)S(1)} %bitcast.300), kind=kOutput, calls=%fused_computation.23 | convolution fusion | flops 5789679616 | bytes 26738688 | tf_op jit(solution)/shard_map/dot_general | solution.py:18
  633.5 21.9 %collective-permute-done.39 = bf16[128,2048]{1,0:T(8,128)(2,1)S(1)} collective-permute-done((bf16[128,2048]{1,0:T(8,128)(2,1)S(1)}, bf16[128,2048]{1,0:T(8,128)(2,1)S(1)}, u32[]{:S(2)}, u32[]{:S(2)}) %collective-permute-start.39) | collective-permute-done | bytes 524320 | tf_op jit(solution)/shard_map/ppermute | solution.py:172
  661.3 12.1 %multiply_convert_fusion = (bf16[1024,1376]{0,1:T(8,128)(2,1)}, bf16[1024,1376]{0,1:T(8,128)(2,1)}) fusion(f32[1024,1376]{0,1:T(8,128)} %fusion.90, f32[1024,1376]{0,1:T(8,128)} %get-tuple-element.344, bf16[1024,2048]{1,0:T(8,128)(2,1)S(1)} %bitcast.288, bf16[2048,1376]{0,1:T(8,128)(2,1)S(1)} %bitcast.302), kind=kOutput, calls=%fused_computation.21 | convolution fusion | flops 5789679616 | bytes 26738688 | tf_op jit(solution)/shard_map/dot_general | solution.py:18
  745.4 14.8 %attend_back0.1 = (bf16[1024,512]{1,0:T(8,128)(2,1)}, f32[1024,512]{1,0:T(8,128)}, f32[1024,512]{1,0:T(8,128)}) custom-call(s32[1]{0:T(128)} %bitcast.31.refs_0_, s32[512,1]{1,0:T(8,128)} %fusion.62.refs_1_, s32[1,512]{1,0:T(1,128)} %fusion.72.refs_2_, bf16[1024,512]{1,0:T(8,128)(2,1)} %convolution_convert_fusion.7.refs_3_, ...), custom_call_target="tpu_custom_call" | custom-call | bytes 65536 | tf_op jit(solution)/shard_map/attend_back0/pallas_call | solution.py:135
  762.9 42.1 %reduce-scatter.6.cloned.1.call-done = bf16[256,1376]{0,1:T(8,128)(2,1)} async-done(((bf16[2048,1376]{0,1:T(8,128)(2,1)}), bf16[256,1376]{0,1:T(8,128)(2,1)}) %reduce-scatter.6.cloned.1.call-update) | async-done | bytes 704528 | tf_op jit(solution)/shard_map/reduce_scatter | solution.py:250
  813.7 23.3 %collective-permute-done.46 = bf16[2,128,2048]{2,1,0:T(8,128)(2,1)S(1)} collective-permute-done((bf16[2,128,2048]{2,1,0:T(8,128)(2,1)S(1)}, bf16[2,128,2048]{2,1,0:T(8,128)(2,1)S(1)}, u32[]{:S(2)}, u32[]{:S(2)}) %collective-permute-start.46) | collective-permute-done | bytes 1048608 | tf_op jit(solution)/shard_map/ppermute | solution.py:163
  881.1 25.8 %attend_back1.1 = (bf16[1024,512]{1,0:T(8,128)(2,1)}, bf16[1024,512]{1,0:T(8,128)(2,1)}, bf16[1024,512]{1,0:T(8,128)(2,1)}, bf16[1024,512]{1,0:T(8,128)(2,1)}, bf16[1024,512]{1,0:T(8,128)(2,1)}) custom-call(s32[1]{0:T(128)} %bitcast.31.refs_0_, s32[512,1]{1,0:T(8,128)} %fusion.62.refs_1_, s32[1,512]{1,0:T(1,128)} %fusion.72.refs_2_, ...), custom_call_target="tpu_custom_call" | custom-call | bytes 65536 | tf_op jit(solution)/shard_map/attend_back1/pallas_call | solution.py:135
  1002.0 17.9 %collective-permute-done.53 = bf16[2,128,2048]{2,1,0:T(8,128)(2,1)S(1)} collective-permute-done((bf16[2,128,2048]{2,1,0:T(8,128)(2,1)S(1)}, bf16[2,128,2048]{2,1,0:T(8,128)(2,1)S(1)}, u32[]{:S(2)}, u32[]{:S(2)}) %collective-permute-start.53) | collective-permute-done | bytes 1048608 | tf_op jit(solution)/shard_map/ppermute | solution.py:163
  1042.5 19.3 %collective-permute-done.55.refs_8_ = bf16[128,2048]{1,0:T(8,128)(2,1)} collective-permute-done((bf16[128,2048]{1,0:T(8,128)(2,1)}, bf16[128,2048]{1,0:T(8,128)(2,1)}, u32[]{:S(2)}, u32[]{:S(2)}) %collective-permute-start.55) | collective-permute-done | bytes 524320 | tf_op jit(solution)/shard_map/ppermute | solution.py:172
  1072.6 19.4 %collective-permute-done.57 = bf16[1024,1536]{1,0:T(8,128)(2,1)} collective-permute-done((bf16[1024,1536]{1,0:T(8,128)(2,1)}, bf16[1024,1536]{1,0:T(8,128)(2,1)}, u32[]{:S(2)}, u32[]{:S(2)}) %collective-permute-start.57) | collective-permute-done | bytes 3145760 | tf_op jit(solution)/shard_map/ppermute | solution.py:167
  1121.3 13.5 %collective-permute-start.67 = (f32[33,128]{1,0:T(8,128)S(1)}, f32[33,128]{1,0:T(8,128)S(1)}, u32[]{:S(2)}, u32[]{:S(2)}) collective-permute-start(f32[33,128]{1,0:T(8,128)S(1)} %add.554), channel_id=1, source_target_pairs={{0,4},{4,0},{8,12},{12,8},{1,5},{5,1},{9,13},{13,9},{2,6},{6,2},{1... | collective-permute-start | bytes 50696 | tf_op jit(solution)/shard_map/ppermute | solution.py:296
  1162.8 24.9 %reduce-scatter.12.cloned.1.call-done = bf16[256,1536]{1,0:T(8,128)(2,1)} async-done(((bf16[1024,1536]{1,0:T(8,128)(2,1)}), bf16[256,1536]{1,0:T(8,128)(2,1)}) %reduce-scatter.12.cloned.1.call-update) | async-done | bytes 786448 | tf_op jit(solution)/shard_map/reduce_scatter | solution.py:645
  (689 shorter events, 663.7 us)
Async XLA Ops:
  7.2 65.2 %all-gather.9.cloned.1.call-start = ((), (), s32[]{:S(2)}) async-start(), calls=%async_computation.5 | async-start | bytes 1392640 | tf_op jit(solution)/shard_map/all_gather | solution.py:375
  10.3 100.5 %all-gather.11.cloned.1.call-start = ((), (), s32[]{:S(2)}) async-start(), calls=%async_computation.6 | async-start | bytes 1310720 | tf_op jit(solution)/shard_map/all_gather | solution.py:375
  17.8 54.5 %collective-permute-start.1 = (bf16[128,2048]{1,0:T(8,128)(2,1)S(1)}, bf16[128,2048]{1,0:T(8,128)(2,1)S(1)}, u32[]{:S(2)}, u32[]{:S(2)}) collective-permute-start(bf16[128,2048]{1,0:T(8,128)(2,1)S(1)} %get-tuple-element.326), channel_id=1, source_target_pairs={{0,8},{4,12},{8,0},{12,4},{1,9},{5,13},{9,1},{13,5},{2,10},{6,14},... | collective-permute-start | bytes 1572872 | tf_op jit(solution)/shard_map/ppermute | solution.py:172
  20.4 51.9 %collective-permute-start.2 = (bf16[128,2048]{1,0:T(8,128)(2,1)S(1)}, bf16[128,2048]{1,0:T(8,128)(2,1)S(1)}, u32[]{:S(2)}, u32[]{:S(2)}) collective-permute-start(bf16[128,2048]{1,0:T(8,128)(2,1)S(1)} %get-tuple-element.325), channel_id=1, source_target_pairs={{0,12},{4,0},{8,4},{12,8},{1,13},{5,1},{9,5},{13,9},{2,14},{6,2},{... | collective-permute-start | bytes 1572872 | tf_op jit(solution)/shard_map/ppermute | solution.py:172
  72.3 67.5 %all-gather.15.cloned.1.call-start = ((), (), s32[]{:S(2)}) async-start(), calls=%async_computation.8 | async-start | bytes 1310720 | tf_op jit(solution)/shard_map/all_gather | solution.py:375
  73.0 103.4 %all-gather.13.cloned.1.call-start = ((), (), s32[]{:S(2)}) async-start(), calls=%async_computation.7 | async-start | bytes 1310720 | tf_op jit(solution)/shard_map/all_gather | solution.py:375
  110.8 134.8 %all-gather.17.cloned.1.call-start = ((), (), s32[]{:S(2)}) async-start(), calls=%async_computation.9 | async-start | bytes 3522560 | tf_op jit(solution)/shard_map/all_gather | solution.py:375
  136.3 48.2 %collective-permute-start.12 = (bf16[1024,512]{1,0:T(8,128)(2,1)}, bf16[1024,512]{1,0:T(8,128)(2,1)}, u32[]{:S(2)}, u32[]{:S(2)}) collective-permute-start(bf16[1024,512]{1,0:T(8,128)(2,1)} %all-gather.11.cloned.1.call-done), channel_id=1, source_target_pairs={{0,16},{16,0},{1,17},{17,1},{2,18},{18,2},{3,19},{19,3},{4,20},{20... | collective-permute-start | bytes 3145736 | tf_op jit(solution)/shard_map/ppermute | solution.py:167
  139.8 205.4 %all-gather.19.cloned.1.call-start = ((), (), s32[]{:S(2)}) async-start(), calls=%async_computation.10 | async-start | bytes 3522560 | tf_op jit(solution)/shard_map/all_gather | solution.py:375
  176.5 243.8 %all-gather.21.cloned.1.call-start = ((), (), s32[]{:S(2)}) async-start(), calls=%async_computation.11 | async-start | bytes 3522560 | tf_op jit(solution)/shard_map/all_gather | solution.py:378
  242.3 92.2 %collective-permute-start.15 = (bf16[2,256,2048]{2,1,0:T(8,128)(2,1)}, bf16[2,256,2048]{2,1,0:T(8,128)(2,1)}, u32[]{:S(2)}, u32[]{:S(2)}) collective-permute-start(bf16[2,256,2048]{2,1,0:T(8,128)(2,1)} %slice.579), channel_id=1, source_target_pairs={{0,1},{1,0},{2,3},{3,2},{4,5},{5,4},{6,7},{7,6},{8,9},{9,8},{10,11... | collective-permute-start | bytes 6291464 | tf_op jit(solution)/shard_map/ppermute | solution.py:159
  245.6 225.6 %all-gather.23.cloned.1.call-start = ((), (), s32[]{:S(2)}) async-start(), calls=%async_computation.12 | async-start | bytes 3522560 | tf_op jit(solution)/shard_map/all_gather | solution.py:378
  255.5 91.2 %collective-permute-start.18 = (bf16[1024,1376]{0,1:T(8,128)(2,1)}, bf16[1024,1376]{0,1:T(8,128)(2,1)}, u32[]{:S(2)}, u32[]{:S(2)}) collective-permute-start(bf16[1024,1376]{0,1:T(8,128)(2,1)} %all-gather.17.cloned.1.call-done), channel_id=1, source_target_pairs={{0,16},{16,0},{1,17},{17,1},{2,18},{18,2},{3,19},{19,3},{4,20},{20... | collective-permute-start | bytes 8454152 | tf_op jit(solution)/shard_map/ppermute | solution.py:167
  278.5 68.2 %collective-permute-start.17 = (bf16[2,256,2048]{2,1,0:T(8,128)(2,1)}, bf16[2,256,2048]{2,1,0:T(8,128)(2,1)}, u32[]{:S(2)}, u32[]{:S(2)}) collective-permute-start(bf16[2,256,2048]{2,1,0:T(8,128)(2,1)} %slice.578), channel_id=1, source_target_pairs={{0,1},{1,0},{2,3},{3,2},{4,5},{5,4},{6,7},{7,6},{8,9},{9,8},{10,11... | collective-permute-start | bytes 6291464 | tf_op jit(solution)/shard_map/ppermute | solution.py:159
  278.7 55.7 %collective-permute-start.27 = (bf16[256,1376]{0,1:T(8,128)(2,1)S(1)}, bf16[256,1376]{0,1:T(8,128)(2,1)}, u32[]{:S(2)}, u32[]{:S(2)}) collective-permute-start(bf16[256,1376]{0,1:T(8,128)(2,1)S(1)} %bitcast.312), channel_id=1, source_target_pairs={{0,16},{16,0},{1,17},{17,1},{2,18},{18,2},{3,19},{19,3},{4,20},{20... | collective-permute-start | bytes 2113544 | tf_op jit(solution)/shard_map/ppermute | solution.py:167
  334.4 470.6 %reduce-scatter.6.cloned.1.call-start = ((), (), s32[]{:S(2)}) async-start(), calls=%async_computation.13 | async-start | bytes 6340608 | tf_op jit(solution)/shard_map/reduce_scatter | solution.py:250
  345.2 73.3 %collective-permute-start.23 = (bf16[1024,1376]{0,1:T(8,128)(2,1)}, bf16[1024,1376]{0,1:T(8,128)(2,1)S(1)}, u32[]{:S(2)}, u32[]{:S(2)}) collective-permute-start(bf16[1024,1376]{0,1:T(8,128)(2,1)} %all-gather.19.cloned.1.call-done), channel_id=1, source_target_pairs={{0,16},{16,0},{1,17},{17,1},{2,18},{18,2},{3,19},{19,3},{4,20},{20... | collective-permute-start | bytes 8454152 | tf_op jit(solution)/shard_map/ppermute | solution.py:167
  686.8 282.9 %reduce-scatter.8.cloned.1.call-start = ((), (), s32[]{:S(2)}) async-start(), calls=%async_computation.14 | async-start | bytes 6340608 | tf_op jit(solution)/shard_map/reduce_scatter | solution.py:250
  843.2 257.0 %reduce-scatter.10.cloned.1.call-start = ((), (), s32[]{:S(2)}) async-start(), calls=%async_computation.15 | async-start | bytes 6340608 | tf_op jit(solution)/shard_map/reduce_scatter | solution.py:250
  942.3 204.0 %reduce-scatter.14.cloned.1.call-start = ((), (), s32[]{:S(2)}) async-start(), calls=%async_computation.17 | async-start | bytes 1310720 | tf_op jit(solution)/shard_map/reduce_scatter | solution.py:535
  999.1 92.9 %collective-permute-start.57 = (bf16[1024,1536]{1,0:T(8,128)(2,1)}, bf16[1024,1536]{1,0:T(8,128)(2,1)}, u32[]{:S(2)}, u32[]{:S(2)}) collective-permute-start(bf16[1024,1536]{1,0:T(8,128)(2,1)} %add_convert_fusion.4), channel_id=1, source_target_pairs={{0,16},{16,0},{1,17},{17,1},{2,18},{18,2},{3,19},{19,3},{4,20},{20... | collective-permute-start | bytes 9437192 | tf_op jit(solution)/shard_map/ppermute | solution.py:167
  1033.1 67.1 %collective-permute-start.60 = (bf16[128,2048]{1,0:T(8,128)(2,1)S(1)}, bf16[128,2048]{1,0:T(8,128)(2,1)}, u32[]{:S(2)}, u32[]{:S(2)}) collective-permute-start(bf16[128,2048]{1,0:T(8,128)(2,1)S(1)} %get-tuple-element.191.refs_0_), channel_id=1, source_target_pairs={{0,2},{1,3},{2,0},{3,1},{4,6},{5,7},{6,4},{7,5},{8,10},{9,11},{10,... | collective-permute-start | bytes 1572872 | tf_op jit(solution)/shard_map/ppermute | solution.py:163
  1034.6 153.1 %reduce-scatter.12.cloned.1.call-start = ((), (), s32[]{:S(2)}) async-start(), calls=%async_computation.16 | async-start | bytes 3932160 | tf_op jit(solution)/shard_map/reduce_scatter | solution.py:645
  1040.9 59.3 %collective-permute-start.61 = (bf16[128,2048]{1,0:T(8,128)(2,1)}, bf16[128,2048]{1,0:T(8,128)(2,1)}, u32[]{:S(2)}, u32[]{:S(2)}) collective-permute-start(bf16[128,2048]{1,0:T(8,128)(2,1)} %collective-permute-done.54.refs_4_), channel_id=1, source_target_pairs={{0,2},{1,3},{2,0},{3,1},{4,6},{5,7},{6,4},{7,5},{8,10},{9,11},{10,... | collective-permute-start | bytes 1572872 | tf_op jit(solution)/shard_map/ppermute | solution.py:163
  (213 other events, 3568.9 us)
Sparse Core Ops, SparseCore 0:
  10.4 59.9 all-gather.8
  72.4 38.2 all-gather.10
  112.3 27.4 all-gather.14
  141.2 29.6 all-gather.12
  172.3 56.3 all-gather.16
  230.2 56.2 all-gather.18
  288.0 56.2 all-gather.20
  345.8 56.2 all-gather.22
  686.9 118.0 reduce-scatter.5
  843.3 116.4 reduce-scatter.7
  963.4 133.1 reduce-scatter.9
  1099.4 26.2 reduce-scatter.13
  1128.1 59.5 reduce-scatter.11
